TPU v7x, 32 devices: a whole 2x2x4 slice. The times are simulated.
32 devices in a mesh: tm: 4 (over y, x), op: 8 (over z, core).
Axes of the slice: x: 2, y: 2, z: 4, core: 2. Of those that a mesh axis runs over, the one named last changes fastest.
Arguments:
- sink_elem: bfloat16 [2, 4, 2048, 16384], P(None, 'tm', 'op'), may hold values from -6 to 6
- source_elem: bfloat16 [2, 2, 2048, 16384], P(None, None, None, 'op'), may hold values from -6 to 6
- peram: bfloat16 [2, 4, 2, 512, 512], P(None, 'tm', None, 'op'), may hold values from -4 to 4
- pair_list: int32 [16, 1], replicated, may hold values from 0 to 15
- spin_sets: int32 [16, 3], replicated, may hold values from 0 to 3
Outputs:
- correlator: float32 [2, 4, 2, 16, 1], P(None, 'tm')
All inputs are finite; a program needn't handle non-finite values.
Results may differ from a plain program's by a relative error of at most 0.0041.
Values may be sent and summed in bfloat16 or wider, within the bound.
No kernel may reach another device: no remote copies, remote signals or barrier semaphores. Data moves between devices by JAX's collectives and lax.ppermute only.
A program may use at most 256 MiB of HBM per device.

v0:
```python
import functools

import jax
import jax.numpy as jnp
from jax import lax
from jax.experimental import pallas as pl
from jax.experimental.pallas import tpu as pltpu
from jax.sharding import PartitionSpec as P


AXES = ("tm", "op")
CORES = 2
EIGHTHS = (2, 2, 2, 1, 1)
ROWS = 16
STEPS = 4
PITCH = ROWS + 1


def complex_matrix(block):
    upper = jnp.concatenate([block[0], block[1]], axis=1)
    lower = jnp.concatenate([-block[1], block[0]], axis=1)
    return jnp.stack([upper, lower])


def baseline_plan(nev, nspin, nop, tsrc, pairs, sink_elem, source_elem, peram, pair_list, spin_sets):
    tau_all = lax.all_gather(peram, "op", axis=3, tiled=True)
    position = lax.axis_index("op")
    rows = sink_elem.shape[2]
    local_times = sink_elem.shape[1]
    span = min(rows, nev)
    groups = rows // span
    cols = source_elem.shape[3]

    def spin_block(local, t0, left, right):
        return lax.dynamic_slice(tau_all[:, local, t0], (0, left * nev, right * nev), (2, nev, nev))

    def sink_side(local, t0, p):
        pieces = []
        for group in range(groups):
            op_now = (position * rows + group * span) // nev
            mine = spin_sets[op_now]
            theirs = spin_sets[pair_list[op_now, p]]
            third = complex_matrix(spin_block(local, t0, mine[2], theirs[2]))
            second = complex_matrix(spin_block(local, t0, mine[1], theirs[1]))
            phi = sink_elem[:, local, group * span : (group + 1) * span].reshape(2, span * nev, nev)
            x_both = jnp.einsum("cxk,ckb->xb", phi, third, preferred_element_type=jnp.float32)
            x_both = x_both.astype(jnp.bfloat16).reshape(span, nev, 2, nev)
            y_both = jnp.einsum("ijck,cjb->ibk", x_both, second, preferred_element_type=jnp.float32)
            y_both = y_both.astype(jnp.bfloat16).reshape(span, 2, nev * nev)
            pieces.append(jnp.transpose(y_both, (1, 0, 2)))
        return jnp.concatenate(pieces, axis=1)

    partial_terms = {}
    for t0 in range(tsrc):
        combos = [(local, t0, p) for local in range(local_times) for p in range(pairs)]
        stacked = jnp.stack([sink_side(local, t0, p) for local, t0, p in combos], axis=1)
        columns = lax.all_to_all(stacked, "op", split_axis=3, concat_axis=2, tiled=True)
        for index, combo in enumerate(combos):
            other = pair_list[:, combo[2]]
            source = source_elem[:, t0].reshape(2, nop, nev, cols)
            chosen = jnp.take(source, other, axis=1)
            tiles = columns[:, index].reshape(2, nop, nev, cols)

            def inner(a, b):
                return jnp.einsum("oic,ojc->oij", a, b, preferred_element_type=jnp.float32)

            m_re = inner(tiles[0], chosen[0]) + inner(tiles[1], chosen[1])
            m_im = inner(tiles[1], chosen[0]) - inner(tiles[0], chosen[1])
            blocks = tau_all[:, combo[0], t0].reshape(2, nspin, nev, nspin, nev)
            blocks = jnp.transpose(blocks, (1, 3, 0, 2, 4))
            first = blocks[spin_sets[:, 0], spin_sets[other, 0]].astype(jnp.float32)
            c_re = jnp.sum(first[:, 0] * m_re - first[:, 1] * m_im, axis=(1, 2))
            c_im = jnp.sum(first[:, 0] * m_im + first[:, 1] * m_re, axis=(1, 2))
            partial_terms[combo] = jnp.stack([c_re, c_im])
    per_local = []
    for local in range(local_times):
        per_time = [
            jnp.stack([partial_terms[local, t0, p] for p in range(pairs)], axis=-1) for t0 in range(tsrc)
        ]
        per_local.append(jnp.stack(per_time, axis=1))
    totals = lax.psum(jnp.stack(per_local, axis=1), "op")
    return totals * (1.0 / float(nev**3))


def spin_kernel(nev, tsrc, held, chips, where_ref, pair_ref, spin_ref, mine_ref, other_ref, *outs):
    t, d = where_ref[0], where_ref[1]
    z, core = d // CORES, d % CORES
    lines = mine_ref.shape[3]
    for e in range(held):
        op_now = d * held + (e + t) % held
        q = pair_ref[op_now, 0]

        def block(n, part, t0):
            a, b = spin_ref[op_now, n], spin_ref[q, n]
            at = pl.multiple_of(b * nev, nev)
            pieces = []
            for piece in range(nev // lines):
                owner = a * (nev // lines) + piece
                r = (z - owner // CORES + chips) % chips
                same = (owner % CORES == core).astype(jnp.float32)
                near = mine_ref[r, part, t0, :, pl.ds(at, nev)].astype(jnp.float32)
                far = other_ref[r, part, t0, :, pl.ds(at, nev)].astype(jnp.float32)
                pieces.append(jnp.where(same > 0.5, near, far))
            return jnp.concatenate(pieces, axis=0)

        for n in range(3):
            for t0 in range(tsrc):
                row = (n * tsrc + t0) * nev
                for part in range(2):
                    outs[e][row : row + nev, part * nev : (part + 1) * nev] = block(n, part, t0).astype(jnp.bfloat16)


def spin_blocks(nev, tsrc, held, chips, where, pair_list, spin_sets, mine, other):
    shape = jax.ShapeDtypeStruct((tsrc * 3 * nev, 2 * nev), jnp.bfloat16)
    smem = pl.BlockSpec(memory_space=pltpu.SMEM)
    vmem = pl.BlockSpec(memory_space=pltpu.VMEM)
    return pl.pallas_call(
        functools.partial(spin_kernel, nev, tsrc, held, chips),
        out_shape=[shape] * held,
        in_specs=[smem, smem, smem, vmem, vmem],
        out_specs=[vmem] * held,
        compiler_params=pltpu.CompilerParams(vmem_limit_bytes=32 << 20),
        name="spins",
    )(where, pair_list, spin_sets, mine, other)


def matrix_kernel(nev, tsrc, held, info_ref, *refs):
    own, came, out_ref = refs[:held], refs[held : 2 * held], refs[-1]
    for e in range(held):

        def block(n, part, t0):
            row = (n * tsrc + t0) * nev
            got = came[e][row : row + nev, part * nev : (part + 1) * nev].astype(jnp.float32)
            if e == 0:
                kept = own[e][row : row + nev, part * nev : (part + 1) * nev].astype(jnp.float32)
                got = jnp.where(info_ref[0] == 1, kept, got)
            return got

        def put(row, left, right):
            out_ref[e, row : row + nev, :nev] = left.astype(jnp.bfloat16)
            out_ref[e, row : row + nev, nev:] = right.astype(jnp.bfloat16)

        for t0 in range(tsrc):
            re, im = block(1, 0, t0).T, block(1, 1, t0).T
            row = t0 * 2 * nev
            put(row, re, -im)
            put(row + nev, im, re)
            re, im = block(2, 0, t0), block(2, 1, t0)
            row = (tsrc + t0) * 2 * nev
            put(row, re, im)
            put(row + nev, -im, re)
            put(tsrc * 4 * nev + t0 * nev, block(0, 0, t0), block(0, 1, t0))


def matrices(nev, tsrc, info, own, came):
    vmem = pl.BlockSpec(memory_space=pltpu.VMEM)
    return pl.pallas_call(
        functools.partial(matrix_kernel, nev, tsrc, len(own)),
        out_shape=jax.ShapeDtypeStruct((len(own), tsrc * 5 * nev, 2 * nev), jnp.bfloat16),
        in_specs=[pl.BlockSpec(memory_space=pltpu.SMEM)] + [vmem] * (2 * len(own)),
        out_specs=vmem,
        compiler_params=pltpu.CompilerParams(vmem_limit_bytes=32 << 20),
        name="matrices",
    )(info, *own, *came)


def mode_kernel(nev, tsrc, held, group, info_ref, own_ref, *refs):
    came, (mats_ref, y_ref, phi, xs, ys, sem) = refs[:held], refs[held:]
    g, steps = pl.program_id(0), pl.num_programs(0) // held

    def fetch(at, slot, act):
        e = at // steps
        line = pl.multiple_of(lax.rem(at, steps) * ROWS, ROWS)
        stays = jnp.logical_and(e == 0, info_ref[0] == 1)

        @pl.when(stays)
        def _():
            mine = pl.multiple_of(info_ref[1] + line, ROWS)
            act(pltpu.make_async_copy(own_ref.at[:, pl.ds(mine, ROWS), :], phi.at[slot], sem.at[slot]))

        for n in range(held):

            @pl.when(jnp.logical_and(e == n, jnp.logical_not(stays)))
            def _():
                act(pltpu.make_async_copy(came[n].at[:, pl.ds(line, ROWS), :], phi.at[slot], sem.at[slot]))

    @pl.when(g == 0)
    def _():
        fetch(0, 0, lambda copy: copy.start())

    slot = lax.rem(g, 2)

    @pl.when(g + 1 < pl.num_programs(0))
    def _():
        fetch(g + 1, 1 - slot, lambda copy: copy.start())

    fetch(g, slot, lambda copy: copy.wait())
    third = jnp.concatenate(
        [mats_ref[0, (tsrc + t0) * 2 * nev : (tsrc + t0 + 1) * 2 * nev, :] for t0 in range(tsrc)], axis=1
    )

    def x_step(step, carry):
        lines = []
        for inner in range(group):
            at = pl.multiple_of((step * group + inner) * nev, nev)
            lines.append(jnp.concatenate([phi[slot, 0, :, pl.ds(at, nev)], phi[slot, 1, :, pl.ds(at, nev)]], axis=1))
        out = jnp.dot(jnp.concatenate(lines, axis=0), third, preferred_element_type=jnp.float32)
        for n in range(2 * tsrc):
            for inner in range(group):
                xs[n, pl.ds((step * group + inner) * PITCH, ROWS), :] = out[
                    inner * ROWS : (inner + 1) * ROWS, n * nev : (n + 1) * nev
                ]
        return carry

    lax.fori_loop(0, nev // group, x_step, 0)

    for t0 in range(tsrc):
        second = mats_ref[0, t0 * 2 * nev : (t0 + 1) * 2 * nev, :]
        for pair in range(0, ROWS, 2):
            sides = []
            for i in (pair, pair + 1):
                halves = [xs[2 * t0 + n, pl.ds(i, nev, stride=PITCH), :].astype(jnp.bfloat16) for n in range(2)]
                sides.append(jnp.concatenate(halves, axis=0))
            out = jnp.dot(second, jnp.concatenate(sides, axis=1), preferred_element_type=jnp.float32)
            for which, i in enumerate((pair, pair + 1)):
                for n in range(2):
                    ys[n, pl.ds(i, nev, stride=PITCH), :] = out[
                        n * nev : (n + 1) * nev, which * nev : (which + 1) * nev
                    ]

        def y_step(step, carry):
            for inner in range(group):
                at = pl.multiple_of((step * group + inner) * nev, nev)
                for n in range(2):
                    y_ref[0, t0, n, :, pl.ds(at, nev)] = ys[n, pl.ds((step * group + inner) * PITCH, ROWS), :].astype(
                        jnp.bfloat16
                    )
            return carry

        lax.fori_loop(0, nev // group, y_step, 0)


def modes(nev, tsrc, info, own, came, mats):
    held = len(came)
    lines, width = came[0].shape[1:]
    steps = lines // ROWS
    hbm = pl.BlockSpec(memory_space=pl.ANY)
    return pl.pallas_call(
        functools.partial(mode_kernel, nev, tsrc, held, 64),
        out_shape=pltpu.HBM((held, tsrc, 2, lines, width), jnp.bfloat16),
        grid=(held * steps,),
        in_specs=[pl.BlockSpec(memory_space=pltpu.SMEM), hbm]
        + [hbm] * held
        + [pl.BlockSpec((1, *mats.shape[1:]), lambda g: (g // steps, 0, 0))],
        out_specs=pl.BlockSpec((1, tsrc, 2, ROWS, width), lambda g: (g // steps, 0, 0, g % steps, 0)),
        scratch_shapes=[
            pltpu.VMEM((2, 2, ROWS, width), jnp.bfloat16),
            pltpu.VMEM((2 * tsrc, nev * PITCH, nev), jnp.float32),
            pltpu.VMEM((2, nev * PITCH, nev), jnp.float32),
            pltpu.SemaphoreType.DMA((2,)),
        ],
        compiler_params=pltpu.CompilerParams(vmem_limit_bytes=48 << 20),
        name="modes",
    )(info, own, *came, mats)


def inner_kernel(nev, tsrc, slots, counts, groups, begin, where_ref, *refs):
    refs = list(refs)

    def take(count):
        got = refs[:count]
        del refs[:count]
        return got

    ys = [[take(len(counts) - first) for _ in range(CORES)] for first in groups]
    sources = [take(CORES) for _ in groups]
    mats_ref, before_ref, out_ref, acc = refs
    lines = acc.shape[1] // (2 * slots)

    @pl.when(pl.program_id(0) == 0)
    def _():
        acc[...] = jnp.zeros_like(acc)

    for t0 in range(tsrc):
        for group, first in enumerate(groups):
            skip = sum(counts[:first])
            total = None
            for block in range(CORES):
                lhs = jnp.concatenate(
                    [piece[slot, t0, n] for slot in range(slots) for n in range(2) for piece in ys[group][block]],
                    axis=0,
                )
                rhs = jnp.concatenate([sources[group][block][n, t0] for n in range(2)], axis=0)
                part = lax.dot_general(lhs, rhs, (((1,), (1,)), ((), ())), preferred_element_type=jnp.float32)
                total = part if total is None else total + part
            if skip == 0:
                acc[t0] += total
            else:
                for part in range(2 * slots):
                    own = lines - skip
                    acc[t0, part * lines + skip : (part + 1) * lines, :] += total[part * own : (part + 1) * own]

    @pl.when(pl.program_id(0) == pl.num_programs(0) - 1)
    def _():
        for slot in range(slots):
            for t0 in range(tsrc):
                row = t0 * nev + begin
                f_re = mats_ref[slot, row : row + lines, :nev].astype(jnp.float32)
                f_im = mats_ref[slot, row : row + lines, nev:].astype(jnp.float32)
                y_re = acc[t0, (2 * slot) * lines : (2 * slot + 1) * lines, :]
                y_im = acc[t0, (2 * slot + 1) * lines : (2 * slot + 2) * lines, :]
                m_re = y_re[:, :nev] + y_im[:, nev:]
                m_im = y_im[:, :nev] - y_re[:, nev:]
                at = (slot * tsrc + t0) * 2
                c_re = jnp.sum(f_re * m_re - f_im * m_im, axis=0, keepdims=True)
                c_im = jnp.sum(f_re * m_im + f_im * m_re, axis=0, keepdims=True)
                out_ref[at : at + 1, :] = before_ref[at : at + 1, :] + c_re
                out_ref[at + 1 : at + 2, :] = before_ref[at + 1 : at + 2, :] + c_im


def inner_products(nev, tsrc, ys, begin, groups, sources, where, mats, before):
    slots = ys[0].shape[0]
    counts = [piece.shape[3] for piece in ys]
    lines = sum(counts)
    args, specs = [], []
    for group, first in enumerate(groups):
        width = sources[group][0].shape[3] // STEPS
        for block in range(CORES):
            for piece in ys[first:]:
                at = group * CORES + block
                args.append(piece)
                specs.append(
                    pl.BlockSpec(
                        (slots, tsrc, 2, piece.shape[3], width), lambda s, w, at=at: (0, 0, 0, 0, w[at] + s)
                    )
                )
    for pair in sources:
        width = pair[0].shape[3] // STEPS
        for piece in pair:
            args.append(pltpu.with_memory_space_constraint(piece, pltpu.HBM))
            specs.append(pl.BlockSpec((2, tsrc, nev, width), lambda s, w: (0, 0, 0, s)))
    args += [mats, before]
    specs.append(pl.BlockSpec((slots, tsrc * nev, 2 * nev), lambda s, w: (0, 4, 0)))
    specs.append(pl.BlockSpec(before.shape, lambda s, w: (0, 0)))
    return pl.pallas_call(
        functools.partial(inner_kernel, nev, tsrc, slots, counts, groups, begin),
        out_shape=jax.ShapeDtypeStruct(before.shape, jnp.float32),
        grid_spec=pltpu.PrefetchScalarGridSpec(
            num_scalar_prefetch=1,
            grid=(STEPS,),
            in_specs=specs,
            out_specs=pl.BlockSpec(before.shape, lambda s, w: (0, 0)),
            scratch_shapes=[pltpu.VMEM((tsrc, slots * 2 * lines, 2 * nev), jnp.float32)],
        ),
        compiler_params=pltpu.CompilerParams(vmem_limit_bytes=56 << 20),
        name="inner",
    )(where, *args)


def chip_plan(nev, nop, tsrc, times, depth, sink_elem, source_elem, peram, pair_list, spin_sets):
    held = sink_elem.shape[2] // nev
    chips = depth // CORES
    t = lax.axis_index("tm")
    d = lax.axis_index("op")
    z, core = d // CORES, d % CORES
    cols = source_elem.shape[3]
    sink = sink_elem[:, 0]

    def over(target):
        pairs = []
        for a in range(times):
            for b in range(depth):
                to, at, side = target(a, b // CORES, b % CORES)
                pairs.append((a * depth + b, to * depth + at * CORES + side))
        return pairs

    def along(r):
        return over(lambda a, b, c: (a, (b + r) % chips, c))

    swap = over(lambda a, b, c: (a, b, (c + 1) % CORES))

    def move(value, pairs):
        return lax.ppermute(value, AXES, pairs)

    own = peram[:, 0]
    mine = [own] + [move(own, along(r)) for r in range(1, chips)]
    mine = jnp.stack(mine)

    def route(e):
        pairs = over(lambda a, b, c: (c * held + (e + a) % held, b, a // held))
        return [pair for pair in pairs if pair[0] != pair[1]]

    stays = core == t // held

    sizes = [nev // 8 * n for n in EIGHTHS]
    begins = [sum(sizes[:n]) for n in range(len(sizes))]

    def send(e, h, after):
        line = (e + t) % held * nev + begins[h]
        piece = lax.dynamic_slice(after, (0, line, 0), (2, sizes[h], after.shape[2]))
        return move(piece, route(e))

    arrived = [[send(e, 0, sink) for e in range(held)]]

    sources = {}
    for name, r, part, parts in rounds(chips):
        q = pair_list[times * ((z + r) % chips) + t, 0]
        width = cols // parts
        piece = lax.dynamic_slice(source_elem, (0, 0, q * nev, part * width), (2, tsrc, nev, width))
        if r:
            piece = move(piece, along(r))
        sources[name] = (piece, move(piece, swap))

    other = move(mine, swap)
    where = jnp.stack([t, d]).astype(jnp.int32)
    made = spin_blocks(nev, tsrc, held, chips, where, pair_list, spin_sets, mine, other)
    info = jnp.stack([stays.astype(jnp.int32), t % held * nev]).astype(jnp.int32)
    mats = matrices(nev, tsrc, info, made, [move(made[e], route(e)) for e in range(held)])
    later, _ = lax.optimization_barrier((sink, mine))
    for h in range(1, len(sizes)):
        arrived.append([send(e, h, later) for e in range(held)])

    ys = []
    for h in range(len(sizes)):
        info = jnp.stack([stays.astype(jnp.int32), t % held * nev + begins[h]]).astype(jnp.int32)
        ys.append(modes(nev, tsrc, info, sink, arrived[h], mats))

    total = jnp.zeros((held * tsrc * 2, nev), jnp.float32)
    places = {}
    for name, r, part, parts in rounds(chips):
        came = (z - r) % chips
        places[name] = [
            ((came * CORES + side) * parts + part) * STEPS for side in (core, (core + 1) % CORES)
        ]
    for name, first, last, cuts, names in products(len(sizes), chips):
        total = inner_products(
            nev,
            tsrc,
            ys[first:last],
            begins[first],
            [cut - first for cut in cuts],
            [sources[n] for n in names],
            jnp.stack([at for n in names for at in places[n]]).astype(jnp.int32),
            mats,
            total,
        )

    plane = []
    for s in range(times):
        pairs = over(lambda a, b, c: (c * held + (a - s) % times // CORES, b, (a - s) % times % CORES))
        plane.append(lax.ppermute(total, AXES, pairs))
    plane = jnp.stack(plane)
    column = jnp.stack([plane] + [lax.ppermute(plane, AXES, along(r)) for r in range(1, chips)])
    values = jnp.sum(column, axis=-1).reshape(chips, times, held, tsrc, 2)
    chip_of = (z - jnp.arange(chips)) % chips
    op_of = (t % held * CORES + core + jnp.arange(times)) % times
    slot_of = (op_of - t) % held
    pick = (
        (jnp.arange(nop)[None, None, None] == (chip_of[:, None] * times + op_of[None])[:, :, None, None])
        & (jnp.arange(held)[None, None, :, None] == slot_of[None, :, None, None])
    )
    values = jnp.where(pick[..., None, None], values[:, :, :, None], 0.0)
    values = jnp.sum(values, axis=(0, 1, 2)) * (1.0 / float(nev**3))
    return jnp.transpose(values, (2, 1, 0))[:, None, :, :, None]


def rounds(chips):
    half = chips // 2
    pieces = [(f"{r}", r, 0, 1) for r in range(half)]
    return pieces + [(f"{r}{'ab'[part]}", r, part, 2) for part in range(2) for r in range(half, chips)]


def products(chunks, chips):
    names = [name for name, *_ in rounds(chips)]
    late = chips - chips // 2
    soon, then, last = names[: chips // 2], names[chips // 2 : -late], names[-late:]
    return [
        ("early", 0, 2, [0] * len(soon), soon),
        ("middle", 0, chunks - 1, [2] * len(soon) + [0] * len(then), soon + then),
        ("last", 0, chunks, [chunks - 1] * len(soon + then) + [0] * len(last), soon + then + last),
    ]


def solution(mesh):
    times, depth = mesh.shape["tm"], mesh.shape["op"]

    def on_device(sink_elem, source_elem, peram, pair_list, spin_sets):
        nop, pairs = pair_list.shape
        nev = source_elem.shape[2] // nop
        nspin = peram.shape[4] // nev
        tsrc = source_elem.shape[1]
        rows = sink_elem.shape[2]
        fits = (
            depth % CORES == 0
            and rows % nev == 0
            and rows // nev * CORES == times
            and sink_elem.shape[1] == 1
            and pairs == 1
            and nev % (8 * ROWS) == 0
            and nev % peram.shape[3] == 0
        )
        if fits:
            return chip_plan(nev, nop, tsrc, times, depth, sink_elem, source_elem, peram, pair_list, spin_sets)
        return baseline_plan(nev, nspin, nop, tsrc, pairs, sink_elem, source_elem, peram, pair_list, spin_sets)

    in_specs = (
        P(None, "tm", "op", None),
        P(None, None, None, "op"),
        P(None, "tm", None, "op", None),
        P(),
        P(),
    )
    out_specs = P(None, "tm", None, None, None)
    return jax.shard_map(on_device, mesh=mesh, in_specs=in_specs, out_specs=out_specs, check_vma=False)
```

profile of v0, /device:TPU:0, one launch (start us, length us, event | category | flops | bytes accessed | tf_op | source)
XLA Modules:
  0.0 452.8 jit_solution(8670637241316324428)
XLA Ops:
  0.0 5.1 %collective-permute-start.2 = (bf16[2,2,64,512]{3,2,1,0:T(8,128)(2,1)}, bf16[2,2,64,512]{3,2,1,0:T(8,128)(2,1)S(1)}, u32[]{:S(2)}, u32[]{:S(2)}) collective-permute-start(bf16[2,2,64,512]{3,2,1,0:T(8,128)(2,1)} %bitcast.55), channel_id=1, source_target_pairs={{0,6},{1,7},{2,0},{3,1},{4,2},{5,3},{6,4},{7,5},{8,14},{9,15},{10,... | collective-permute-start | bytes 786440 | tf_op jit(solution)/shard_map/ppermute | solution.py:383
  8.8 4.3 constant_dynamic-slice_fusion
  17.9 33.3 %collective-permute-done.1 = bf16[2,2,64,512]{3,2,1,0:T(8,128)(2,1)S(1)} collective-permute-done((bf16[2,2,64,512]{3,2,1,0:T(8,128)(2,1)}, bf16[2,2,64,512]{3,2,1,0:T(8,128)(2,1)S(1)}, u32[]{:S(2)}, u32[]{:S(2)}) %collective-permute-start.1) | collective-permute-done | bytes 262176 | tf_op jit(solution)/shard_map/ppermute | solution.py:383
  51.5 4.3 constant_dynamic-slice_fusion.10
  55.7 40.5 %collective-permute-done.19.refs_28_.refs_32_ = bf16[2,2,128,1024]{3,2,1,0:T(8,128)(2,1)S(1)} collective-permute-done((bf16[2,2,128,1024]{3,2,1,0:T(8,128)(2,1)}, bf16[2,2,128,1024]{3,2,1,0:T(8,128)(2,1)S(1)}, u32[]{:S(2)}, u32[]{:S(2)}) %collective-permute-start.19) | collective-permute-done | bytes 1048608 | tf_op jit(solution)/shard_map/ppermute | solution.py:383
  99.5 41.7 %collective-permute-done.23.refs_36_ = bf16[2,2,128,1024]{3,2,1,0:T(8,128)(2,1)S(1)} collective-permute-done((bf16[2,2,128,1024]{3,2,1,0:T(8,128)(2,1)}, bf16[2,2,128,1024]{3,2,1,0:T(8,128)(2,1)S(1)}, u32[]{:S(2)}, u32[]{:S(2)}) %collective-permute-start.23) | collective-permute-done | bytes 1048608 | tf_op jit(solution)/shard_map/ppermute | solution.py:383
  144.4 4.6 %dynamic-slice_bitcast_fusion = (bf16[2,32,16384]{2,1,0:T(8,128)(2,1)}, bf16[2,32,16384]{2,1,0:T(8,128)(2,1)}) fusion(bf16[2,1,256,16384]{3,2,1,0:T(8,128)(2,1)} %param.5, s32[]{:T(128)S(6)} %select_n.212, s32[]{:T(128)S(6)} %select_n.211), kind=kLoop, calls=%fused_computation | loop fusion | bytes 8388616 | tf_op jit(solution)/shard_map/dynamic_slice | solution.py:400
  153.4 4.8 %constant_dynamic-slice_fusion.6 = (bf16[2,2,128,2048]{3,2,1,0:T(8,128)(2,1)}, bf16[2,2,128,2048]{3,2,1,0:T(8,128)(2,1)}) fusion(bf16[2,2,2048,2048]{3,2,1,0:T(8,128)(2,1)} %param.6, s32[]{:T(128)S(6)} %select_n.223, s32[]{:T(128)S(6)} %select_n.220), kind=kLoop, calls=%fused_computation.14 | loop fusion | bytes 8388616 | tf_op jit(solution)/shard_map/dynamic_slice | solution.py:409
  159.6 7.1 %collective-permute-start.16 = (bf16[2,2,128,2048]{3,2,1,0:T(8,128)(2,1)}, bf16[2,2,128,2048]{3,2,1,0:T(8,128)(2,1)}, u32[]{:S(2)}, u32[]{:S(2)}) collective-permute-start(bf16[2,2,128,2048]{3,2,1,0:T(8,128)(2,1)} %get-tuple-element.16.refs_8_.refs_24_.refs_28_), channel_id=1, source_target_pairs={{0,1},{1,0},{2,3},{3,2},{4,5},{5,4},{6,7},{7,6},{8,9},{9,8},{10,11... | collective-permute-start | bytes 6291464 | tf_op jit(solution)/shard_map/ppermute | solution.py:383
  168.5 23.6 %collective-permute-start.17 = (bf16[2,2,128,2048]{3,2,1,0:T(8,128)(2,1)}, bf16[2,2,128,2048]{3,2,1,0:T(8,128)(2,1)}, u32[]{:S(2)}, u32[]{:S(2)}) collective-permute-start(bf16[2,2,128,2048]{3,2,1,0:T(8,128)(2,1)} %get-tuple-element.15), channel_id=1, source_target_pairs={{0,2},{1,3},{2,4},{3,5},{4,6},{5,7},{6,0},{7,1},{8,10},{9,11},{10,... | collective-permute-start | bytes 6291464 | tf_op jit(solution)/shard_map/ppermute | solution.py:383
  193.6 6.9 %constant_dynamic-slice_fusion.12 = (bf16[2,32,16384]{2,1,0:T(8,128)(2,1)}, bf16[2,32,16384]{2,1,0:T(8,128)(2,1)}, bf16[2,32,16384]{2,1,0:T(8,128)(2,1)}, bf16[2,32,16384]{2,1,0:T(8,128)(2,1)}) fusion(bf16[2,256,16384]{2,1,0:T(8,128)(2,1)} %bitcast.49, s32[]{:T(128)S(6)} %select_n.216, s32[]{:T(128)S(6)} %select_n.215, s32[]{:T(128)S(6)} %select_n.214, ...), kind=kLoop, calls=%fused_computation.20 | loop fusion | bytes 16777232 | tf_op jit(solution)/shard_map/dynamic_slice | solution.py:400
  200.5 21.3 %collective-permute-done.7.refs_3_ = bf16[768,256]{1,0:T(8,128)(2,1)S(1)} collective-permute-done((bf16[768,256]{1,0:T(8,128)(2,1)}, bf16[768,256]{1,0:T(8,128)(2,1)S(1)}, u32[]{:S(2)}, u32[]{:S(2)}) %collective-permute-start.7) | collective-permute-done | bytes 393248 | tf_op jit(solution)/shard_map/ppermute | solution.py:383
  228.6 12.1 %collective-permute-done.17.refs_10_.refs_26_.refs_30_ = bf16[2,2,128,2048]{3,2,1,0:T(8,128)(2,1)} collective-permute-done((bf16[2,2,128,2048]{3,2,1,0:T(8,128)(2,1)}, bf16[2,2,128,2048]{3,2,1,0:T(8,128)(2,1)}, u32[]{:S(2)}, u32[]{:S(2)}) %collective-permute-start.17) | collective-permute-done | bytes 2097184 | tf_op jit(solution)/shard_map/ppermute | solution.py:383
  241.4 29.9 %collective-permute-start.20 = (bf16[2,2,128,1024]{3,2,1,0:T(8,128)(2,1)}, bf16[2,2,128,1024]{3,2,1,0:T(8,128)(2,1)}, u32[]{:S(2)}, u32[]{:S(2)}) collective-permute-start(bf16[2,2,128,1024]{3,2,1,0:T(8,128)(2,1)} %copy-done.5), channel_id=1, source_target_pairs={{0,1},{1,0},{2,3},{3,2},{4,5},{5,4},{6,7},{7,6},{8,9},{9,8},{10,11... | collective-permute-start | bytes 3145736 | tf_op jit(solution)/shard_map/ppermute | solution.py:383
  276.0 42.2 %collective-permute-start.24 = (bf16[2,2,128,1024]{3,2,1,0:T(8,128)(2,1)}, bf16[2,2,128,1024]{3,2,1,0:T(8,128)(2,1)}, u32[]{:S(2)}, u32[]{:S(2)}) collective-permute-start(bf16[2,2,128,1024]{3,2,1,0:T(8,128)(2,1)} %copy-done.6), channel_id=1, source_target_pairs={{0,1},{1,0},{2,3},{3,2},{4,5},{5,4},{6,7},{7,6},{8,9},{9,8},{10,11... | collective-permute-start | bytes 3145736 | tf_op jit(solution)/shard_map/ppermute | solution.py:383
  324.8 7.5 %modes.5.refs_0_.refs_1_.refs_2_.refs_3_.refs_4_.refs_5_.refs_6_.refs_7_.refs_12_.refs_17_.refs_22_.refs_27_ = bf16[2,2,2,16,16384]{4,3,2,1,0:T(8,128)(2,1)} custom-call(s32[2]{0:T(128)S(1)} %get-tuple-element.35.info_ref, bf16[2,256,16384]{2,1,0:T(8,128)(2,1)} %bitcast.50, bf16[2,16,16384]{2,1,0:T(8,128)(2,1)S(1)} %collective-permute-done.3.refs_0_, ...), custom_call_target="tpu_custom_call" | custom-call | tf_op jit(solution)/shard_map/modes/pallas_call | solution.py:248
  332.3 7.4 %modes.9.refs_1_.refs_3_.refs_5_.refs_7_.refs_11_.refs_15_.refs_19_.refs_23_.refs_16_.refs_21_.refs_26_ = bf16[2,2,2,16,16384]{4,3,2,1,0:T(8,128)(2,1)} custom-call(s32[2]{0:T(128)S(1)} %pad_add_fusion.5.info_ref, bf16[2,256,16384]{2,1,0:T(8,128)(2,1)} %bitcast.51, bf16[2,16,16384]{2,1,0:T(8,128)(2,1)} %collective-permute-done.14.refs_0_, ...), custom_call_target="tpu_custom_call" | custom-call | tf_op jit(solution)/shard_map/modes/pallas_call | solution.py:248
  339.7 11.9 %modes.6.refs_0_.refs_2_.refs_4_.refs_6_.refs_8_.refs_12_.refs_16_.refs_20_.refs_13_.refs_18_.refs_23_ = bf16[2,2,2,32,16384]{4,3,2,1,0:T(8,128)(2,1)} custom-call(s32[2]{0:T(128)S(1)} %get-tuple-element.36.info_ref, bf16[2,256,16384]{2,1,0:T(8,128)(2,1)} %bitcast.52, bf16[2,32,16384]{2,1,0:T(8,128)(2,1)S(1)} %collective-permute-done.8.refs_0_, ...), custom_call_target="tpu_custom_call" | custom-call | tf_op jit(solution)/shard_map/modes/pallas_call | solution.py:248
  351.6 11.9 %modes.7.refs_1_.refs_3_.refs_5_.refs_7_.refs_9_.refs_13_.refs_17_.refs_21_.refs_14_.refs_19_.refs_24_ = bf16[2,2,2,32,16384]{4,3,2,1,0:T(8,128)(2,1)} custom-call(s32[2]{0:T(128)S(1)} %get-tuple-element.37.info_ref, bf16[2,256,16384]{2,1,0:T(8,128)(2,1)} %bitcast.53, bf16[2,32,16384]{2,1,0:T(8,128)(2,1)} %collective-permute-done.10.refs_0_, ...), custom_call_target="tpu_custom_call" | custom-call | tf_op jit(solution)/shard_map/modes/pallas_call | solution.py:248
  363.5 11.9 %modes.8.refs_0_.refs_2_.refs_4_.refs_6_.refs_10_.refs_14_.refs_18_.refs_22_.refs_15_.refs_20_.refs_25_ = bf16[2,2,2,32,16384]{4,3,2,1,0:T(8,128)(2,1)} custom-call(s32[2]{0:T(128)S(1)} %get-tuple-element.38.info_ref, bf16[2,256,16384]{2,1,0:T(8,128)(2,1)} %bitcast.54, bf16[2,32,16384]{2,1,0:T(8,128)(2,1)} %collective-permute-done.12.refs_0_, ...), custom_call_target="tpu_custom_call" | custom-call | tf_op jit(solution)/shard_map/modes/pallas_call | solution.py:248
  376.0 8.9 %inner.3.refs_33_ = f32[8,128]{1,0:T(8,128)} custom-call(s32[4]{0:T(128)} %pad_add_fusion.6.where_ref, bf16[2,2,2,32,16384]{4,3,2,1,0:T(8,128)(2,1)} %modes.6.refs_0_.refs_2_.refs_4_.refs_6_.refs_8_.refs_12_.refs_16_.refs_20_.refs_13_.refs_18_.refs_23_, ...), custom_call_target="tpu_custom_call" | custom-call | tf_op jit(solution)/shard_map/inner/pallas_call | solution.py:345
  384.9 12.8 %inner.4.refs_41_ = f32[8,128]{1,0:T(8,128)} custom-call(s32[8]{0:T(128)} %stack.183.where_ref, bf16[2,2,2,32,16384]{4,3,2,1,0:T(8,128)(2,1)} %modes.8.refs_0_.refs_2_.refs_4_.refs_6_.refs_10_.refs_14_.refs_18_.refs_22_.refs_15_.refs_20_.refs_25_, ...), custom_call_target="tpu_custom_call" | custom-call | tf_op jit(solution)/shard_map/inner/pallas_call | solution.py:345
  397.8 14.2 %inner.5 = f32[8,128]{1,0:T(8,128)} custom-call(s32[12]{0:T(128)} %stack.163.where_ref, bf16[2,2,2,16,16384]{4,3,2,1,0:T(8,128)(2,1)} %modes.5.refs_0_.refs_1_.refs_2_.refs_3_.refs_4_.refs_5_.refs_6_.refs_7_.refs_12_.refs_17_.refs_22_.refs_27_, ...), custom_call_target="tpu_custom_call" | custom-call | tf_op jit(solution)/shard_map/inner/pallas_call | solution.py:345
  420.5 25.8 %collective-permute-start.33 = (f32[4,8,128]{2,1,0:T(8,128)S(1)}, f32[4,8,128]{2,1,0:T(8,128)S(1)}, u32[]{:S(2)}, u32[]{:S(2)}) collective-permute-start(f32[4,8,128]{2,1,0:T(8,128)S(1)} %get-tuple-element.28), channel_id=1, source_target_pairs={{0,6},{1,7},{2,0},{3,1},{4,2},{5,3},{6,4},{7,5},{8,14},{9,15},{10,... | collective-permute-start | bytes 49160 | tf_op jit(solution)/shard_map/ppermute | solution.py:453
  (107 shorter events, 56.1 us)
Async XLA Ops:
  5.1 46.2 %collective-permute-start.1 = (bf16[2,2,64,512]{3,2,1,0:T(8,128)(2,1)}, bf16[2,2,64,512]{3,2,1,0:T(8,128)(2,1)S(1)}, u32[]{:S(2)}, u32[]{:S(2)}) collective-permute-start(bf16[2,2,64,512]{3,2,1,0:T(8,128)(2,1)} %bitcast.56), channel_id=1, source_target_pairs={{0,4},{1,5},{2,6},{3,7},{4,0},{5,1},{6,2},{7,3},{8,12},{9,13},{10,... | collective-permute-start | bytes 786440 | tf_op jit(solution)/shard_map/ppermute | solution.py:383
  5.1 46.2 %collective-permute-start = (bf16[2,2,64,512]{3,2,1,0:T(8,128)(2,1)}, bf16[2,2,64,512]{3,2,1,0:T(8,128)(2,1)S(1)}, u32[]{:S(2)}, u32[]{:S(2)}) collective-permute-start(bf16[2,2,64,512]{3,2,1,0:T(8,128)(2,1)} %bitcast.57), channel_id=1, source_target_pairs={{0,2},{1,3},{2,4},{3,5},{4,6},{5,7},{6,0},{7,1},{8,10},{9,11},{10,... | collective-permute-start | bytes 786440 | tf_op jit(solution)/shard_map/ppermute | solution.py:383
  13.1 83.1 %collective-permute-start.19 = (bf16[2,2,128,1024]{3,2,1,0:T(8,128)(2,1)}, bf16[2,2,128,1024]{3,2,1,0:T(8,128)(2,1)S(1)}, u32[]{:S(2)}, u32[]{:S(2)}) collective-permute-start(bf16[2,2,128,1024]{3,2,1,0:T(8,128)(2,1)} %get-tuple-element.13), channel_id=1, source_target_pairs={{0,4},{1,5},{2,6},{3,7},{4,0},{5,1},{6,2},{7,3},{8,12},{9,13},{10,... | collective-permute-start | bytes 3145736 | tf_op jit(solution)/shard_map/ppermute | solution.py:383
  15.0 82.9 %collective-permute-start.21 = (bf16[2,2,128,1024]{3,2,1,0:T(8,128)(2,1)}, bf16[2,2,128,1024]{3,2,1,0:T(8,128)(2,1)}, u32[]{:S(2)}, u32[]{:S(2)}) collective-permute-start(bf16[2,2,128,1024]{3,2,1,0:T(8,128)(2,1)} %get-tuple-element.12), channel_id=1, source_target_pairs={{0,6},{1,7},{2,0},{3,1},{4,2},{5,3},{6,4},{7,5},{8,14},{9,15},{10,... | collective-permute-start | bytes 3145736 | tf_op jit(solution)/shard_map/ppermute | solution.py:383
  17.9 123.2 %collective-permute-start.23 = (bf16[2,2,128,1024]{3,2,1,0:T(8,128)(2,1)}, bf16[2,2,128,1024]{3,2,1,0:T(8,128)(2,1)S(1)}, u32[]{:S(2)}, u32[]{:S(2)}) collective-permute-start(bf16[2,2,128,1024]{3,2,1,0:T(8,128)(2,1)} %get-tuple-element.14), channel_id=1, source_target_pairs={{0,4},{1,5},{2,6},{3,7},{4,0},{5,1},{6,2},{7,3},{8,12},{9,13},{10,... | collective-permute-start | bytes 3145736 | tf_op jit(solution)/shard_map/ppermute | solution.py:383
  51.2 100.7 %collective-permute-start.25 = (bf16[2,2,128,1024]{3,2,1,0:T(8,128)(2,1)}, bf16[2,2,128,1024]{3,2,1,0:T(8,128)(2,1)}, u32[]{:S(2)}, u32[]{:S(2)}) collective-permute-start(bf16[2,2,128,1024]{3,2,1,0:T(8,128)(2,1)} %get-tuple-element.11), channel_id=1, source_target_pairs={{0,6},{1,7},{2,0},{3,1},{4,2},{5,3},{6,4},{7,5},{8,14},{9,15},{10,... | collective-permute-start | bytes 3145736 | tf_op jit(solution)/shard_map/ppermute | solution.py:383
  51.4 91.4 %collective-permute-start.5 = (bf16[4,2,2,64,512]{4,3,2,1,0:T(8,128)(2,1)S(1)}, bf16[4,2,2,64,512]{4,3,2,1,0:T(8,128)(2,1)S(1)}, u32[]{:S(2)}, u32[]{:S(2)}) collective-permute-start(bf16[4,2,2,64,512]{4,3,2,1,0:T(8,128)(2,1)S(1)} %pad_maximum_fusion.mine_ref), channel_id=1, source_target_pairs={{0,1},{1,0},{2,3},{3,2},{4,5},{5,4},{6,7},{7,6},{8,9},{9,8},{10,11... | collective-permute-start | bytes 3145736 | tf_op jit(solution)/shard_map/ppermute | solution.py:383
  97.2 61.0 %collective-permute-start.3 = (bf16[2,16,16384]{2,1,0:T(8,128)(2,1)}, bf16[2,16,16384]{2,1,0:T(8,128)(2,1)S(1)}, u32[]{:S(2)}, u32[]{:S(2)}) collective-permute-start(bf16[2,16,16384]{2,1,0:T(8,128)(2,1)} %get-tuple-element.20), channel_id=1, source_target_pairs={{1,16},{3,18},{5,20},{7,22},{9,24},{11,26},{13,28},{15,30},{16,1},... | collective-permute-start | bytes 3145736 | tf_op jit(solution)/shard_map/ppermute | solution.py:383
  97.9 61.1 %collective-permute-start.4 = (bf16[2,16,16384]{2,1,0:T(8,128)(2,1)}, bf16[2,16,16384]{2,1,0:T(8,128)(2,1)}, u32[]{:S(2)}, u32[]{:S(2)}) collective-permute-start(bf16[2,16,16384]{2,1,0:T(8,128)(2,1)} %get-tuple-element.19), channel_id=1, source_target_pairs={{0,8},{1,24},{2,10},{3,26},{4,12},{5,28},{6,14},{7,30},{8,0},{9,16... | collective-permute-start | bytes 3145736 | tf_op jit(solution)/shard_map/ppermute | solution.py:383
  152.0 40.1 %collective-permute-start.6 = (bf16[768,256]{1,0:T(8,128)(2,1)S(1)}, bf16[768,256]{1,0:T(8,128)(2,1)}, u32[]{:S(2)}, u32[]{:S(2)}) collective-permute-start(bf16[768,256]{1,0:T(8,128)(2,1)S(1)} %get-tuple-element.9.refs_0_), channel_id=1, source_target_pairs={{1,16},{3,18},{5,20},{7,22},{9,24},{11,26},{13,28},{15,30},{16,1},... | collective-permute-start | bytes 1179656 | tf_op jit(solution)/shard_map/ppermute | solution.py:383
  158.2 66.3 %collective-permute-start.8 = (bf16[2,32,16384]{2,1,0:T(8,128)(2,1)}, bf16[2,32,16384]{2,1,0:T(8,128)(2,1)S(1)}, u32[]{:S(2)}, u32[]{:S(2)}) collective-permute-start(bf16[2,32,16384]{2,1,0:T(8,128)(2,1)} %get-tuple-element.26), channel_id=1, source_target_pairs={{1,16},{3,18},{5,20},{7,22},{9,24},{11,26},{13,28},{15,30},{16,1},... | collective-permute-start | bytes 6291464 | tf_op jit(solution)/shard_map/ppermute | solution.py:383
  159.0 67.0 %collective-permute-start.9 = (bf16[2,32,16384]{2,1,0:T(8,128)(2,1)}, bf16[2,32,16384]{2,1,0:T(8,128)(2,1)}, u32[]{:S(2)}, u32[]{:S(2)}) collective-permute-start(bf16[2,32,16384]{2,1,0:T(8,128)(2,1)} %get-tuple-element.25), channel_id=1, source_target_pairs={{0,8},{1,24},{2,10},{3,26},{4,12},{5,28},{6,14},{7,30},{8,0},{9,16... | collective-permute-start | bytes 6291464 | tf_op jit(solution)/shard_map/ppermute | solution.py:383
  159.6 68.4 %collective-permute-start.16 = (bf16[2,2,128,2048]{3,2,1,0:T(8,128)(2,1)}, bf16[2,2,128,2048]{3,2,1,0:T(8,128)(2,1)}, u32[]{:S(2)}, u32[]{:S(2)}) collective-permute-start(bf16[2,2,128,2048]{3,2,1,0:T(8,128)(2,1)} %get-tuple-element.16.refs_8_.refs_24_.refs_28_), channel_id=1, source_target_pairs={{0,1},{1,0},{2,3},{3,2},{4,5},{5,4},{6,7},{7,6},{8,9},{9,8},{10,11... | collective-permute-start | bytes 6291464 | tf_op jit(solution)/shard_map/ppermute | solution.py:383
  168.5 72.1 %collective-permute-start.17 = (bf16[2,2,128,2048]{3,2,1,0:T(8,128)(2,1)}, bf16[2,2,128,2048]{3,2,1,0:T(8,128)(2,1)}, u32[]{:S(2)}, u32[]{:S(2)}) collective-permute-start(bf16[2,2,128,2048]{3,2,1,0:T(8,128)(2,1)} %get-tuple-element.15), channel_id=1, source_target_pairs={{0,2},{1,3},{2,4},{3,5},{4,6},{5,7},{6,0},{7,1},{8,10},{9,11},{10,... | collective-permute-start | bytes 6291464 | tf_op jit(solution)/shard_map/ppermute | solution.py:383
  192.1 29.7 %collective-permute-start.7 = (bf16[768,256]{1,0:T(8,128)(2,1)}, bf16[768,256]{1,0:T(8,128)(2,1)S(1)}, u32[]{:S(2)}, u32[]{:S(2)}) collective-permute-start(bf16[768,256]{1,0:T(8,128)(2,1)} %copy-done.1), channel_id=1, source_target_pairs={{0,8},{1,24},{2,10},{3,26},{4,12},{5,28},{6,14},{7,30},{8,0},{9,16... | collective-permute-start | bytes 1179656 | tf_op jit(solution)/shard_map/ppermute | solution.py:383
  224.5 47.8 %collective-permute-start.11 = (bf16[2,32,16384]{2,1,0:T(8,128)(2,1)}, bf16[2,32,16384]{2,1,0:T(8,128)(2,1)}, u32[]{:S(2)}, u32[]{:S(2)}) collective-permute-start(bf16[2,32,16384]{2,1,0:T(8,128)(2,1)} %get-tuple-element.23), channel_id=1, source_target_pairs={{0,8},{1,24},{2,10},{3,26},{4,12},{5,28},{6,14},{7,30},{8,0},{9,16... | collective-permute-start | bytes 6291464 | tf_op jit(solution)/shard_map/ppermute | solution.py:383
  226.1 49.9 %collective-permute-start.12 = (bf16[2,32,16384]{2,1,0:T(8,128)(2,1)}, bf16[2,32,16384]{2,1,0:T(8,128)(2,1)}, u32[]{:S(2)}, u32[]{:S(2)}) collective-permute-start(bf16[2,32,16384]{2,1,0:T(8,128)(2,1)} %get-tuple-element.22), channel_id=1, source_target_pairs={{1,16},{3,18},{5,20},{7,22},{9,24},{11,26},{13,28},{15,30},{16,1},... | collective-permute-start | bytes 6291464 | tf_op jit(solution)/shard_map/ppermute | solution.py:383
  228.1 90.1 %collective-permute-start.13 = (bf16[2,32,16384]{2,1,0:T(8,128)(2,1)}, bf16[2,32,16384]{2,1,0:T(8,128)(2,1)}, u32[]{:S(2)}, u32[]{:S(2)}) collective-permute-start(bf16[2,32,16384]{2,1,0:T(8,128)(2,1)} %get-tuple-element.21), channel_id=1, source_target_pairs={{0,8},{1,24},{2,10},{3,26},{4,12},{5,28},{6,14},{7,30},{8,0},{9,16... | collective-permute-start | bytes 6291464 | tf_op jit(solution)/shard_map/ppermute | solution.py:383
  240.6 134.8 %collective-permute-start.18 = (bf16[2,2,128,2048]{3,2,1,0:T(8,128)(2,1)}, bf16[2,2,128,2048]{3,2,1,0:T(8,128)(2,1)}, u32[]{:S(2)}, u32[]{:S(2)}) collective-permute-start(bf16[2,2,128,2048]{3,2,1,0:T(8,128)(2,1)} %collective-permute-done.17.refs_10_.refs_26_.refs_30_), channel_id=1, source_target_pairs={{0,1},{1,0},{2,3},{3,2},{4,5},{5,4},{6,7},{7,6},{8,9},{9,8},{10,11... | collective-permute-start | bytes 6291464 | tf_op jit(solution)/shard_map/ppermute | solution.py:383
  241.4 143.5 %collective-permute-start.20 = (bf16[2,2,128,1024]{3,2,1,0:T(8,128)(2,1)}, bf16[2,2,128,1024]{3,2,1,0:T(8,128)(2,1)}, u32[]{:S(2)}, u32[]{:S(2)}) collective-permute-start(bf16[2,2,128,1024]{3,2,1,0:T(8,128)(2,1)} %copy-done.5), channel_id=1, source_target_pairs={{0,1},{1,0},{2,3},{3,2},{4,5},{5,4},{6,7},{7,6},{8,9},{9,8},{10,11... | collective-permute-start | bytes 3145736 | tf_op jit(solution)/shard_map/ppermute | solution.py:383
  272.3 112.6 %collective-permute-start.22 = (bf16[2,2,128,1024]{3,2,1,0:T(8,128)(2,1)}, bf16[2,2,128,1024]{3,2,1,0:T(8,128)(2,1)}, u32[]{:S(2)}, u32[]{:S(2)}) collective-permute-start(bf16[2,2,128,1024]{3,2,1,0:T(8,128)(2,1)} %collective-permute-done.21.refs_30_.refs_34_), channel_id=1, source_target_pairs={{0,1},{1,0},{2,3},{3,2},{4,5},{5,4},{6,7},{7,6},{8,9},{9,8},{10,11... | collective-permute-start | bytes 3145736 | tf_op jit(solution)/shard_map/ppermute | solution.py:383
  276.0 121.8 %collective-permute-start.24 = (bf16[2,2,128,1024]{3,2,1,0:T(8,128)(2,1)}, bf16[2,2,128,1024]{3,2,1,0:T(8,128)(2,1)}, u32[]{:S(2)}, u32[]{:S(2)}) collective-permute-start(bf16[2,2,128,1024]{3,2,1,0:T(8,128)(2,1)} %copy-done.6), channel_id=1, source_target_pairs={{0,1},{1,0},{2,3},{3,2},{4,5},{5,4},{6,7},{7,6},{8,9},{9,8},{10,11... | collective-permute-start | bytes 3145736 | tf_op jit(solution)/shard_map/ppermute | solution.py:383
  318.2 79.6 %collective-permute-start.26 = (bf16[2,2,128,1024]{3,2,1,0:T(8,128)(2,1)}, bf16[2,2,128,1024]{3,2,1,0:T(8,128)(2,1)}, u32[]{:S(2)}, u32[]{:S(2)}) collective-permute-start(bf16[2,2,128,1024]{3,2,1,0:T(8,128)(2,1)} %collective-permute-done.25.refs_38_), channel_id=1, source_target_pairs={{0,1},{1,0},{2,3},{3,2},{4,5},{5,4},{6,7},{7,6},{8,9},{9,8},{10,11... | collective-permute-start | bytes 3145736 | tf_op jit(solution)/shard_map/ppermute | solution.py:383
  420.5 27.3 %collective-permute-start.33 = (f32[4,8,128]{2,1,0:T(8,128)S(1)}, f32[4,8,128]{2,1,0:T(8,128)S(1)}, u32[]{:S(2)}, u32[]{:S(2)}) collective-permute-start(f32[4,8,128]{2,1,0:T(8,128)S(1)} %get-tuple-element.28), channel_id=1, source_target_pairs={{0,6},{1,7},{2,0},{3,1},{4,2},{5,3},{6,4},{7,5},{8,14},{9,15},{10,... | collective-permute-start | bytes 49160 | tf_op jit(solution)/shard_map/ppermute | solution.py:453
  (22 other events, 291.2 us)
where the time goes:
time: 456 us; the launch traced here: 453 us
  starting transfers between devices  169 us (37%)
  waiting for transfers between devices  157 us (34%)
  Pallas kernels  89.1 us (20%)
  local copies, waits for them, and re-layouts  32.7 us (7%)
    ppermute x27, waiting for transfers between devices, move(): return lax.ppermute(value, AXES, pairs)  152 us
    ppermute x27, starting transfers between devices, move(): return lax.ppermute(value, AXES, pairs)  134 us
    pallas_call x5, Pallas kernels, modes(): pl.pallas_call(functools.partial(mode_kernel, nev, tsrc, held, 64), out_s...  50.6 us
    pallas_call x3, Pallas kernels, inner_products(): pl.pallas_call(functools.partial(inner_kernel, nev, tsrc, slots, counts,...  35.9 us
    ppermute x3, starting transfers between devices, chip_plan(): lax.ppermute(plane, AXES, along(r))  26.5 us
    dynamic_slice x3, local copies, waits for them, and re-layouts, send(): lax.dynamic_slice(after, (0, line, 0), (2, sizes[h], after.shape[2]))  15.8 us
  transfers between devices with their start and end apart: 34, of which 11 were waited for; matrix products, arithmetic and copies ran while one was open for 7% of the time, Pallas kernels for 17%

commit v1 on v0

--- a/solution.py
+++ b/solution.py
@@ -445,23 +445,17 @@
             total,
         )
 
-    plane = []
-    for s in range(times):
-        pairs = over(lambda a, b, c: (c * held + (a - s) % times // CORES, b, (a - s) % times % CORES))
-        plane.append(lax.ppermute(total, AXES, pairs))
-    plane = jnp.stack(plane)
-    column = jnp.stack([plane] + [lax.ppermute(plane, AXES, along(r)) for r in range(1, chips)])
-    values = jnp.sum(column, axis=-1).reshape(chips, times, held, tsrc, 2)
-    chip_of = (z - jnp.arange(chips)) % chips
-    op_of = (t % held * CORES + core + jnp.arange(times)) % times
-    slot_of = (op_of - t) % held
-    pick = (
-        (jnp.arange(nop)[None, None, None] == (chip_of[:, None] * times + op_of[None])[:, :, None, None])
-        & (jnp.arange(held)[None, None, :, None] == slot_of[None, :, None, None])
+    spread = jnp.broadcast_to(total[None], (times * depth, *total.shape))
+    spread = lax.all_to_all(spread, AXES, 0, 0, tiled=True)
+    values = jnp.sum(spread, axis=-1).reshape(times, chips, CORES, held, tsrc, 2)
+    slot_of = (jnp.arange(times) - t) % held
+    pick = (jnp.arange(held)[None, None] == slot_of[:, None, None]) & (
+        jnp.arange(CORES)[None, :, None] == t // held
     )
-    values = jnp.where(pick[..., None, None], values[:, :, :, None], 0.0)
-    values = jnp.sum(values, axis=(0, 1, 2)) * (1.0 / float(nev**3))
-    return jnp.transpose(values, (2, 1, 0))[:, None, :, :, None]
+    values = jnp.where(pick[:, None, :, :, None, None], values, 0.0)
+    values = jnp.sum(values, axis=(2, 3)) * (1.0 / float(nev**3))
+    values = jnp.transpose(values, (3, 2, 1, 0)).reshape(2, 1, tsrc, nop, 1)
+    return values
 
 
 def rounds(chips):
@@ -476,7 +470,8 @@
     soon, then, last = names[: chips // 2], names[chips // 2 : -late], names[-late:]
     return [
         ("early", 0, 2, [0] * len(soon), soon),
-        ("middle", 0, chunks - 1, [2] * len(soon) + [0] * len(then), soon + then),
+        ("next", 2, chunks - 2, [2] * len(soon), soon),
+        ("middle", 0, chunks - 1, [chunks - 2] * len(soon) + [0] * len(then), soon + then),
         ("last", 0, chunks, [chunks - 1] * len(soon + then) + [0] * len(last), soon + then + last),
     ]
 

time: 456 us -> 461 us (1.011)
  starting transfers between devices: 169 us -> 159 us
  Pallas kernels: 89.1 us -> 97.2 us
  waiting for transfers between devices: 157 us -> 164 us
    ppermute x7 -> x0, starting transfers between devices: 34.6 us -> none  [the longest x3 26.5 us: chip_plan(): lax.ppermute(plane, AXES, along(r))]
    all_to_all x0 -> x1, starting transfers between devices: none -> 27.5 us  [chip_plan(): spread = lax.all_to_all(spread, AXES, 0, 0, tiled=True)]
    all_to_all x0 -> x1, waiting for transfers between devices: none -> 8.06 us  [chip_plan(): spread = lax.all_to_all(spread, AXES, 0, 0, tiled=True)]
    pallas_call x3 -> x4, Pallas kernels: 35.9 us -> 42.8 us  [inner_products(): pl.pallas_call(functools.partial(inner_kernel, nev, tsrc, slots, counts,...]
    ppermute x7 -> x0, waiting for transfers between devices: 5.17 us -> none  [the longest x3 4.82 us: chip_plan(): lax.ppermute(plane, AXES, along(r))]
  transfers between devices with their start and end apart: 34 -> 28, of which waited for: 11 -> 7; matrix products, arithmetic and copies ran while one was open for 7% -> 6% of each run, Pallas kernels for 17% -> 18%
where the time goes in v1:
time: 461 us; the launch traced here: 460 us
  waiting for transfers between devices  164 us (36%)
  starting transfers between devices  159 us (34%)
  Pallas kernels  97.2 us (21%)
  local copies, waits for them, and re-layouts  35.7 us (8%)
    ppermute x27, waiting for transfers between devices, move(): return lax.ppermute(value, AXES, pairs)  156 us
    ppermute x27, starting transfers between devices, move(): return lax.ppermute(value, AXES, pairs)  131 us
    pallas_call x5, Pallas kernels, modes(): pl.pallas_call(functools.partial(mode_kernel, nev, tsrc, held, 64), out_s...  51.7 us
    pallas_call x4, Pallas kernels, inner_products(): pl.pallas_call(functools.partial(inner_kernel, nev, tsrc, slots, counts,...  42.8 us
    all_to_all x1, starting transfers between devices, chip_plan(): spread = lax.all_to_all(spread, AXES, 0, 0, tiled=True)  27.5 us
    dynamic_slice x3, local copies, waits for them, and re-layouts, send(): lax.dynamic_slice(after, (0, line, 0), (2, sizes[h], after.shape[2]))  12.8 us
  transfers between devices with their start and end apart: 28, of which 7 were waited for; matrix products, arithmetic and copies ran while one was open for 6% of the time, Pallas kernels for 18%

profile of v1, /device:TPU:0, one launch (start us, length us, event | category | flops | bytes accessed | tf_op | source)
XLA Modules:
  0.0 460.2 jit_solution(11822302102150356702)
XLA Ops:
  0.0 5.1 %collective-permute-start.2 = (bf16[2,2,64,512]{3,2,1,0:T(8,128)(2,1)}, bf16[2,2,64,512]{3,2,1,0:T(8,128)(2,1)S(1)}, u32[]{:S(2)}, u32[]{:S(2)}) collective-permute-start(bf16[2,2,64,512]{3,2,1,0:T(8,128)(2,1)} %bitcast.46), channel_id=1, source_target_pairs={{0,6},{1,7},{2,0},{3,1},{4,2},{5,3},{6,4},{7,5},{8,14},{9,15},{10,... | collective-permute-start | bytes 786440 | tf_op jit(solution)/shard_map/ppermute | solution.py:383
  17.8 33.4 %collective-permute-done.1 = bf16[2,2,64,512]{3,2,1,0:T(8,128)(2,1)S(1)} collective-permute-done((bf16[2,2,64,512]{3,2,1,0:T(8,128)(2,1)}, bf16[2,2,64,512]{3,2,1,0:T(8,128)(2,1)S(1)}, u32[]{:S(2)}, u32[]{:S(2)}) %collective-permute-start.1) | collective-permute-done | bytes 262176 | tf_op jit(solution)/shard_map/ppermute | solution.py:383
  51.5 4.2 constant_dynamic-slice_fusion.10
  55.7 40.6 %collective-permute-done.19.refs_24_.refs_32_ = bf16[2,2,128,1024]{3,2,1,0:T(8,128)(2,1)} collective-permute-done((bf16[2,2,128,1024]{3,2,1,0:T(8,128)(2,1)S(1)}, bf16[2,2,128,1024]{3,2,1,0:T(8,128)(2,1)}, u32[]{:S(2)}, u32[]{:S(2)}) %collective-permute-start.19) | collective-permute-done | bytes 1048608 | tf_op jit(solution)/shard_map/ppermute | solution.py:383
  98.6 42.6 %collective-permute-done.23.refs_36_ = bf16[2,2,128,1024]{3,2,1,0:T(8,128)(2,1)} collective-permute-done((bf16[2,2,128,1024]{3,2,1,0:T(8,128)(2,1)}, bf16[2,2,128,1024]{3,2,1,0:T(8,128)(2,1)}, u32[]{:S(2)}, u32[]{:S(2)}) %collective-permute-start.23) | collective-permute-done | bytes 1048608 | tf_op jit(solution)/shard_map/ppermute | solution.py:383
  144.5 4.6 dynamic-slice_bitcast_fusion
  153.4 4.8 %constant_dynamic-slice_fusion.6 = (bf16[2,2,128,2048]{3,2,1,0:T(8,128)(2,1)}, bf16[2,2,128,2048]{3,2,1,0:T(8,128)(2,1)}) fusion(bf16[2,2,2048,2048]{3,2,1,0:T(8,128)(2,1)} %param.6, s32[]{:T(128)S(6)} %select_n.200, s32[]{:T(128)S(6)} %select_n.197), kind=kLoop, calls=%fused_computation.11 | loop fusion | bytes 8388616 | tf_op jit(solution)/shard_map/dynamic_slice | solution.py:409
  159.6 7.3 %collective-permute-start.16 = (bf16[2,2,128,2048]{3,2,1,0:T(8,128)(2,1)}, bf16[2,2,128,2048]{3,2,1,0:T(8,128)(2,1)}, u32[]{:S(2)}, u32[]{:S(2)}) collective-permute-start(bf16[2,2,128,2048]{3,2,1,0:T(8,128)(2,1)} %get-tuple-element.16.refs_8_.refs_4_.refs_20_.refs_28_), channel_id=1, source_target_pairs={{0,1},{1,0},{2,3},{3,2},{4,5},{5,4},{6,7},{7,6},{8,9},{9,8},{10,11... | collective-permute-start | bytes 6291464 | tf_op jit(solution)/shard_map/ppermute | solution.py:383
  168.6 22.1 %collective-permute-start.17 = (bf16[2,2,128,2048]{3,2,1,0:T(8,128)(2,1)}, bf16[2,2,128,2048]{3,2,1,0:T(8,128)(2,1)}, u32[]{:S(2)}, u32[]{:S(2)}) collective-permute-start(bf16[2,2,128,2048]{3,2,1,0:T(8,128)(2,1)} %get-tuple-element.15), channel_id=1, source_target_pairs={{0,2},{1,3},{2,4},{3,5},{4,6},{5,7},{6,0},{7,1},{8,10},{9,11},{10,... | collective-permute-start | bytes 6291464 | tf_op jit(solution)/shard_map/ppermute | solution.py:383
  196.3 25.6 %collective-permute-done.7.refs_3_ = bf16[768,256]{1,0:T(8,128)(2,1)S(1)} collective-permute-done((bf16[768,256]{1,0:T(8,128)(2,1)}, bf16[768,256]{1,0:T(8,128)(2,1)S(1)}, u32[]{:S(2)}, u32[]{:S(2)}) %collective-permute-start.7) | collective-permute-done | bytes 393248 | tf_op jit(solution)/shard_map/ppermute | solution.py:383
  226.4 11.7 %collective-permute-done.17.refs_10_.refs_6_.refs_22_.refs_30_ = bf16[2,2,128,2048]{3,2,1,0:T(8,128)(2,1)} collective-permute-done((bf16[2,2,128,2048]{3,2,1,0:T(8,128)(2,1)}, bf16[2,2,128,2048]{3,2,1,0:T(8,128)(2,1)}, u32[]{:S(2)}, u32[]{:S(2)}) %collective-permute-start.17) | collective-permute-done | bytes 2097184 | tf_op jit(solution)/shard_map/ppermute | solution.py:383
  241.6 30.9 %collective-permute-start.20 = (bf16[2,2,128,1024]{3,2,1,0:T(8,128)(2,1)}, bf16[2,2,128,1024]{3,2,1,0:T(8,128)(2,1)}, u32[]{:S(2)}, u32[]{:S(2)}) collective-permute-start(bf16[2,2,128,1024]{3,2,1,0:T(8,128)(2,1)} %collective-permute-done.19.refs_24_.refs_32_), channel_id=1, source_target_pairs={{0,1},{1,0},{2,3},{3,2},{4,5},{5,4},{6,7},{7,6},{8,9},{9,8},{10,11... | collective-permute-start | bytes 3145736 | tf_op jit(solution)/shard_map/ppermute | solution.py:383
  278.4 40.9 %collective-permute-start.24 = (bf16[2,2,128,1024]{3,2,1,0:T(8,128)(2,1)}, bf16[2,2,128,1024]{3,2,1,0:T(8,128)(2,1)}, u32[]{:S(2)}, u32[]{:S(2)}) collective-permute-start(bf16[2,2,128,1024]{3,2,1,0:T(8,128)(2,1)} %collective-permute-done.23.refs_36_), channel_id=1, source_target_pairs={{0,1},{1,0},{2,3},{3,2},{4,5},{5,4},{6,7},{7,6},{8,9},{9,8},{10,11... | collective-permute-start | bytes 3145736 | tf_op jit(solution)/shard_map/ppermute | solution.py:383
  326.7 7.7 %modes.5.refs_0_.refs_1_.refs_2_.refs_3_.refs_4_.refs_5_.refs_6_.refs_7_.refs_12_.refs_17_.refs_22_.refs_27_ = bf16[2,2,2,16,16384]{4,3,2,1,0:T(8,128)(2,1)} custom-call(s32[2]{0:T(128)S(1)} %get-tuple-element.31.info_ref, bf16[2,256,16384]{2,1,0:T(8,128)(2,1)} %bitcast.41, bf16[2,16,16384]{2,1,0:T(8,128)(2,1)S(1)} %collective-permute-done.3.refs_0_, ...), custom_call_target="tpu_custom_call" | custom-call | tf_op jit(solution)/shard_map/modes/pallas_call | solution.py:248
  334.4 7.4 %modes.9.refs_0_.refs_1_.refs_2_.refs_3_.refs_7_.refs_11_.refs_15_.refs_19_.refs_16_.refs_21_.refs_26_ = bf16[2,2,2,16,16384]{4,3,2,1,0:T(8,128)(2,1)} custom-call(s32[2]{0:T(128)S(1)} %pad_add_fusion.5.info_ref, bf16[2,256,16384]{2,1,0:T(8,128)(2,1)} %bitcast.42, bf16[2,16,16384]{2,1,0:T(8,128)(2,1)} %collective-permute-done.14.refs_0_, ...), custom_call_target="tpu_custom_call" | custom-call | tf_op jit(solution)/shard_map/modes/pallas_call | solution.py:248
  341.8 12.2 %modes.6.refs_0_.refs_2_.refs_4_.refs_6_.refs_8_.refs_12_.refs_16_.refs_13_.refs_18_.refs_23_ = bf16[2,2,2,32,16384]{4,3,2,1,0:T(8,128)(2,1)} custom-call(s32[2]{0:T(128)S(1)} %get-tuple-element.32.info_ref, bf16[2,256,16384]{2,1,0:T(8,128)(2,1)} %bitcast.43, bf16[2,32,16384]{2,1,0:T(8,128)(2,1)S(1)} %collective-permute-done.8.refs_0_, ...), custom_call_target="tpu_custom_call" | custom-call | tf_op jit(solution)/shard_map/modes/pallas_call | solution.py:248
  354.1 12.3 %modes.7.refs_1_.refs_3_.refs_5_.refs_7_.refs_9_.refs_13_.refs_17_.refs_14_.refs_19_.refs_24_ = bf16[2,2,2,32,16384]{4,3,2,1,0:T(8,128)(2,1)} custom-call(s32[2]{0:T(128)S(1)} %get-tuple-element.33.info_ref, bf16[2,256,16384]{2,1,0:T(8,128)(2,1)} %bitcast.44, bf16[2,32,16384]{2,1,0:T(8,128)(2,1)S(1)} %copy-done.2, bf16[2,32,16384]{2,1,0:T(8,128)(2,1)S(1)} %copy-done.4, ...), custom_call_target="tpu_custom_call" | custom-call | tf_op jit(solution)/shard_map/modes/pallas_call | solution.py:248
  366.5 12.0 %modes.8.refs_0_.refs_1_.refs_2_.refs_3_.refs_6_.refs_10_.refs_14_.refs_18_.refs_15_.refs_20_.refs_25_ = bf16[2,2,2,32,16384]{4,3,2,1,0:T(8,128)(2,1)} custom-call(s32[2]{0:T(128)S(1)} %get-tuple-element.34.info_ref, bf16[2,256,16384]{2,1,0:T(8,128)(2,1)} %bitcast.45, bf16[2,32,16384]{2,1,0:T(8,128)(2,1)S(1)} %copy-done.6, ...), custom_call_target="tpu_custom_call" | custom-call | tf_op jit(solution)/shard_map/modes/pallas_call | solution.py:248
  379.1 8.9 %inner.4.refs_9_ = f32[8,128]{1,0:T(8,128)} custom-call(s32[4]{0:T(128)} %pad_add_fusion.6.where_ref, bf16[2,2,2,32,16384]{4,3,2,1,0:T(8,128)(2,1)} %modes.6.refs_0_.refs_2_.refs_4_.refs_6_.refs_8_.refs_12_.refs_16_.refs_13_.refs_18_.refs_23_, ...), custom_call_target="tpu_custom_call" | custom-call | tf_op jit(solution)/shard_map/inner/pallas_call | solution.py:345
  388.0 8.0 %inner.5.refs_29_ = f32[8,128]{1,0:T(8,128)} custom-call(s32[4]{0:T(128)} %pad_add_fusion.6.where_ref, bf16[2,2,2,32,16384]{4,3,2,1,0:T(8,128)(2,1)} %modes.8.refs_0_.refs_1_.refs_2_.refs_3_.refs_6_.refs_10_.refs_14_.refs_18_.refs_15_.refs_20_.refs_25_, ...), custom_call_target="tpu_custom_call" | custom-call | tf_op jit(solution)/shard_map/inner/pallas_call | solution.py:345
  396.0 11.8 %inner.6.refs_41_ = f32[8,128]{1,0:T(8,128)} custom-call(s32[8]{0:T(128)} %stack.158.where_ref, bf16[2,2,2,16,16384]{4,3,2,1,0:T(8,128)(2,1)} %modes.9.refs_0_.refs_1_.refs_2_.refs_3_.refs_7_.refs_11_.refs_15_.refs_19_.refs_16_.refs_21_.refs_26_, ...), custom_call_target="tpu_custom_call" | custom-call | tf_op jit(solution)/shard_map/inner/pallas_call | solution.py:345
  407.8 14.2 %inner.7 = f32[8,128]{1,0:T(8,128)} custom-call(s32[12]{0:T(128)} %stack.138.where_ref, bf16[2,2,2,16,16384]{4,3,2,1,0:T(8,128)(2,1)} %modes.5.refs_0_.refs_1_.refs_2_.refs_3_.refs_4_.refs_5_.refs_6_.refs_7_.refs_12_.refs_17_.refs_22_.refs_27_, ...), custom_call_target="tpu_custom_call" | custom-call | tf_op jit(solution)/shard_map/inner/pallas_call | solution.py:345
  423.4 27.5 %all-to-all-start = ((f32[32,8,128]{2,1,0:T(8,128)}), f32[32,8,128]{2,1,0:T(8,128)S(1)}, u32[]{:S(2)}, u32[]{:S(2)}) async-start(f32[32,8,128]{2,1,0:T(8,128)} %broadcast_in_dim.27), calls=%async_computation | async-start | bytes 262144 | tf_op jit(solution)/shard_map/all_to_all | solution.py:449
  451.0 8.1 %all-to-all-done = f32[32,8,128]{2,1,0:T(8,128)S(1)} async-done(((f32[32,8,128]{2,1,0:T(8,128)}), f32[32,8,128]{2,1,0:T(8,128)S(1)}, u32[]{:S(2)}, u32[]{:S(2)}) %all-to-all-start) | async-done | bytes 131104 | tf_op jit(solution)/shard_map/all_to_all | solution.py:449
  (106 shorter events, 53.3 us)
Async XLA Ops:
  5.1 46.2 %collective-permute-start.1 = (bf16[2,2,64,512]{3,2,1,0:T(8,128)(2,1)}, bf16[2,2,64,512]{3,2,1,0:T(8,128)(2,1)S(1)}, u32[]{:S(2)}, u32[]{:S(2)}) collective-permute-start(bf16[2,2,64,512]{3,2,1,0:T(8,128)(2,1)} %bitcast.47), channel_id=1, source_target_pairs={{0,4},{1,5},{2,6},{3,7},{4,0},{5,1},{6,2},{7,3},{8,12},{9,13},{10,... | collective-permute-start | bytes 786440 | tf_op jit(solution)/shard_map/ppermute | solution.py:383
  5.1 46.2 %collective-permute-start = (bf16[2,2,64,512]{3,2,1,0:T(8,128)(2,1)}, bf16[2,2,64,512]{3,2,1,0:T(8,128)(2,1)S(1)}, u32[]{:S(2)}, u32[]{:S(2)}) collective-permute-start(bf16[2,2,64,512]{3,2,1,0:T(8,128)(2,1)} %bitcast.48), channel_id=1, source_target_pairs={{0,2},{1,3},{2,4},{3,5},{4,6},{5,7},{6,0},{7,1},{8,10},{9,11},{10,... | collective-permute-start | bytes 786440 | tf_op jit(solution)/shard_map/ppermute | solution.py:383
  12.9 83.4 %collective-permute-start.19 = (bf16[2,2,128,1024]{3,2,1,0:T(8,128)(2,1)S(1)}, bf16[2,2,128,1024]{3,2,1,0:T(8,128)(2,1)}, u32[]{:S(2)}, u32[]{:S(2)}) collective-permute-start(bf16[2,2,128,1024]{3,2,1,0:T(8,128)(2,1)S(1)} %get-tuple-element.13), channel_id=1, source_target_pairs={{0,4},{1,5},{2,6},{3,7},{4,0},{5,1},{6,2},{7,3},{8,12},{9,13},{10,... | collective-permute-start | bytes 3145736 | tf_op jit(solution)/shard_map/ppermute | solution.py:383
  14.9 82.2 %collective-permute-start.21 = (bf16[2,2,128,1024]{3,2,1,0:T(8,128)(2,1)}, bf16[2,2,128,1024]{3,2,1,0:T(8,128)(2,1)}, u32[]{:S(2)}, u32[]{:S(2)}) collective-permute-start(bf16[2,2,128,1024]{3,2,1,0:T(8,128)(2,1)} %get-tuple-element.12), channel_id=1, source_target_pairs={{0,6},{1,7},{2,0},{3,1},{4,2},{5,3},{6,4},{7,5},{8,14},{9,15},{10,... | collective-permute-start | bytes 3145736 | tf_op jit(solution)/shard_map/ppermute | solution.py:383
  17.8 123.5 %collective-permute-start.23 = (bf16[2,2,128,1024]{3,2,1,0:T(8,128)(2,1)}, bf16[2,2,128,1024]{3,2,1,0:T(8,128)(2,1)}, u32[]{:S(2)}, u32[]{:S(2)}) collective-permute-start(bf16[2,2,128,1024]{3,2,1,0:T(8,128)(2,1)} %get-tuple-element.14), channel_id=1, source_target_pairs={{0,4},{1,5},{2,6},{3,7},{4,0},{5,1},{6,2},{7,3},{8,12},{9,13},{10,... | collective-permute-start | bytes 3145736 | tf_op jit(solution)/shard_map/ppermute | solution.py:383
  51.2 100.8 %collective-permute-start.25 = (bf16[2,2,128,1024]{3,2,1,0:T(8,128)(2,1)}, bf16[2,2,128,1024]{3,2,1,0:T(8,128)(2,1)}, u32[]{:S(2)}, u32[]{:S(2)}) collective-permute-start(bf16[2,2,128,1024]{3,2,1,0:T(8,128)(2,1)} %get-tuple-element.11), channel_id=1, source_target_pairs={{0,6},{1,7},{2,0},{3,1},{4,2},{5,3},{6,4},{7,5},{8,14},{9,15},{10,... | collective-permute-start | bytes 3145736 | tf_op jit(solution)/shard_map/ppermute | solution.py:383
  51.4 91.6 %collective-permute-start.5 = (bf16[4,2,2,64,512]{4,3,2,1,0:T(8,128)(2,1)S(1)}, bf16[4,2,2,64,512]{4,3,2,1,0:T(8,128)(2,1)S(1)}, u32[]{:S(2)}, u32[]{:S(2)}) collective-permute-start(bf16[4,2,2,64,512]{4,3,2,1,0:T(8,128)(2,1)S(1)} %pad_maximum_fusion.mine_ref), channel_id=1, source_target_pairs={{0,1},{1,0},{2,3},{3,2},{4,5},{5,4},{6,7},{7,6},{8,9},{9,8},{10,11... | collective-permute-start | bytes 3145736 | tf_op jit(solution)/shard_map/ppermute | solution.py:383
  96.3 61.9 %collective-permute-start.3 = (bf16[2,16,16384]{2,1,0:T(8,128)(2,1)}, bf16[2,16,16384]{2,1,0:T(8,128)(2,1)S(1)}, u32[]{:S(2)}, u32[]{:S(2)}) collective-permute-start(bf16[2,16,16384]{2,1,0:T(8,128)(2,1)} %get-tuple-element.20), channel_id=1, source_target_pairs={{1,16},{3,18},{5,20},{7,22},{9,24},{11,26},{13,28},{15,30},{16,1},... | collective-permute-start | bytes 3145736 | tf_op jit(solution)/shard_map/ppermute | solution.py:383
  97.1 62.0 %collective-permute-start.4 = (bf16[2,16,16384]{2,1,0:T(8,128)(2,1)}, bf16[2,16,16384]{2,1,0:T(8,128)(2,1)}, u32[]{:S(2)}, u32[]{:S(2)}) collective-permute-start(bf16[2,16,16384]{2,1,0:T(8,128)(2,1)} %get-tuple-element.19), channel_id=1, source_target_pairs={{0,8},{1,24},{2,10},{3,26},{4,12},{5,28},{6,14},{7,30},{8,0},{9,16... | collective-permute-start | bytes 3145736 | tf_op jit(solution)/shard_map/ppermute | solution.py:383
  152.0 38.7 %collective-permute-start.6 = (bf16[768,256]{1,0:T(8,128)(2,1)S(1)}, bf16[768,256]{1,0:T(8,128)(2,1)}, u32[]{:S(2)}, u32[]{:S(2)}) collective-permute-start(bf16[768,256]{1,0:T(8,128)(2,1)S(1)} %get-tuple-element.9.refs_0_), channel_id=1, source_target_pairs={{1,16},{3,18},{5,20},{7,22},{9,24},{11,26},{13,28},{15,30},{16,1},... | collective-permute-start | bytes 1179656 | tf_op jit(solution)/shard_map/ppermute | solution.py:383
  158.2 65.2 %collective-permute-start.8 = (bf16[2,32,16384]{2,1,0:T(8,128)(2,1)}, bf16[2,32,16384]{2,1,0:T(8,128)(2,1)S(1)}, u32[]{:S(2)}, u32[]{:S(2)}) collective-permute-start(bf16[2,32,16384]{2,1,0:T(8,128)(2,1)} %get-tuple-element.26), channel_id=1, source_target_pairs={{1,16},{3,18},{5,20},{7,22},{9,24},{11,26},{13,28},{15,30},{16,1},... | collective-permute-start | bytes 6291464 | tf_op jit(solution)/shard_map/ppermute | solution.py:383
  159.0 66.0 %collective-permute-start.9 = (bf16[2,32,16384]{2,1,0:T(8,128)(2,1)}, bf16[2,32,16384]{2,1,0:T(8,128)(2,1)}, u32[]{:S(2)}, u32[]{:S(2)}) collective-permute-start(bf16[2,32,16384]{2,1,0:T(8,128)(2,1)} %get-tuple-element.25), channel_id=1, source_target_pairs={{0,8},{1,24},{2,10},{3,26},{4,12},{5,28},{6,14},{7,30},{8,0},{9,16... | collective-permute-start | bytes 6291464 | tf_op jit(solution)/shard_map/ppermute | solution.py:383
  159.6 66.2 %collective-permute-start.16 = (bf16[2,2,128,2048]{3,2,1,0:T(8,128)(2,1)}, bf16[2,2,128,2048]{3,2,1,0:T(8,128)(2,1)}, u32[]{:S(2)}, u32[]{:S(2)}) collective-permute-start(bf16[2,2,128,2048]{3,2,1,0:T(8,128)(2,1)} %get-tuple-element.16.refs_8_.refs_4_.refs_20_.refs_28_), channel_id=1, source_target_pairs={{0,1},{1,0},{2,3},{3,2},{4,5},{5,4},{6,7},{7,6},{8,9},{9,8},{10,11... | collective-permute-start | bytes 6291464 | tf_op jit(solution)/shard_map/ppermute | solution.py:383
  168.6 69.5 %collective-permute-start.17 = (bf16[2,2,128,2048]{3,2,1,0:T(8,128)(2,1)}, bf16[2,2,128,2048]{3,2,1,0:T(8,128)(2,1)}, u32[]{:S(2)}, u32[]{:S(2)}) collective-permute-start(bf16[2,2,128,2048]{3,2,1,0:T(8,128)(2,1)} %get-tuple-element.15), channel_id=1, source_target_pairs={{0,2},{1,3},{2,4},{3,5},{4,6},{5,7},{6,0},{7,1},{8,10},{9,11},{10,... | collective-permute-start | bytes 6291464 | tf_op jit(solution)/shard_map/ppermute | solution.py:383
  190.7 31.1 %collective-permute-start.7 = (bf16[768,256]{1,0:T(8,128)(2,1)}, bf16[768,256]{1,0:T(8,128)(2,1)S(1)}, u32[]{:S(2)}, u32[]{:S(2)}) collective-permute-start(bf16[768,256]{1,0:T(8,128)(2,1)} %copy-done.9), channel_id=1, source_target_pairs={{0,8},{1,24},{2,10},{3,26},{4,12},{5,28},{6,14},{7,30},{8,0},{9,16... | collective-permute-start | bytes 1179656 | tf_op jit(solution)/shard_map/ppermute | solution.py:383
  223.4 49.1 %collective-permute-start.11 = (bf16[2,32,16384]{2,1,0:T(8,128)(2,1)S(1)}, bf16[2,32,16384]{2,1,0:T(8,128)(2,1)S(1)}, u32[]{:S(2)}, u32[]{:S(2)}) collective-permute-start(bf16[2,32,16384]{2,1,0:T(8,128)(2,1)S(1)} %get-tuple-element.23), channel_id=1, source_target_pairs={{0,8},{1,24},{2,10},{3,26},{4,12},{5,28},{6,14},{7,30},{8,0},{9,16... | collective-permute-start | bytes 6291464 | tf_op jit(solution)/shard_map/ppermute | solution.py:383
  225.0 52.0 %collective-permute-start.12 = (bf16[2,32,16384]{2,1,0:T(8,128)(2,1)S(1)}, bf16[2,32,16384]{2,1,0:T(8,128)(2,1)S(1)}, u32[]{:S(2)}, u32[]{:S(2)}) collective-permute-start(bf16[2,32,16384]{2,1,0:T(8,128)(2,1)S(1)} %get-tuple-element.22), channel_id=1, source_target_pairs={{1,16},{3,18},{5,20},{7,22},{9,24},{11,26},{13,28},{15,30},{16,1},... | collective-permute-start | bytes 6291464 | tf_op jit(solution)/shard_map/ppermute | solution.py:383
  225.8 93.5 %collective-permute-start.13 = (bf16[2,32,16384]{2,1,0:T(8,128)(2,1)S(1)}, bf16[2,32,16384]{2,1,0:T(8,128)(2,1)S(1)}, u32[]{:S(2)}, u32[]{:S(2)}) collective-permute-start(bf16[2,32,16384]{2,1,0:T(8,128)(2,1)S(1)} %get-tuple-element.21), channel_id=1, source_target_pairs={{0,8},{1,24},{2,10},{3,26},{4,12},{5,28},{6,14},{7,30},{8,0},{9,16... | collective-permute-start | bytes 6291464 | tf_op jit(solution)/shard_map/ppermute | solution.py:383
  238.1 140.4 %collective-permute-start.18 = (bf16[2,2,128,2048]{3,2,1,0:T(8,128)(2,1)}, bf16[2,2,128,2048]{3,2,1,0:T(8,128)(2,1)}, u32[]{:S(2)}, u32[]{:S(2)}) collective-permute-start(bf16[2,2,128,2048]{3,2,1,0:T(8,128)(2,1)} %collective-permute-done.17.refs_10_.refs_6_.refs_22_.refs_30_), channel_id=1, source_target_pairs={{0,1},{1,0},{2,3},{3,2},{4,5},{5,4},{6,7},{7,6},{8,9},{9,8},{10,11... | collective-permute-start | bytes 6291464 | tf_op jit(solution)/shard_map/ppermute | solution.py:383
  241.6 154.4 %collective-permute-start.20 = (bf16[2,2,128,1024]{3,2,1,0:T(8,128)(2,1)}, bf16[2,2,128,1024]{3,2,1,0:T(8,128)(2,1)}, u32[]{:S(2)}, u32[]{:S(2)}) collective-permute-start(bf16[2,2,128,1024]{3,2,1,0:T(8,128)(2,1)} %collective-permute-done.19.refs_24_.refs_32_), channel_id=1, source_target_pairs={{0,1},{1,0},{2,3},{3,2},{4,5},{5,4},{6,7},{7,6},{8,9},{9,8},{10,11... | collective-permute-start | bytes 3145736 | tf_op jit(solution)/shard_map/ppermute | solution.py:383
  273.8 122.2 %collective-permute-start.22 = (bf16[2,2,128,1024]{3,2,1,0:T(8,128)(2,1)}, bf16[2,2,128,1024]{3,2,1,0:T(8,128)(2,1)}, u32[]{:S(2)}, u32[]{:S(2)}) collective-permute-start(bf16[2,2,128,1024]{3,2,1,0:T(8,128)(2,1)} %collective-permute-done.21.refs_26_.refs_34_), channel_id=1, source_target_pairs={{0,1},{1,0},{2,3},{3,2},{4,5},{5,4},{6,7},{7,6},{8,9},{9,8},{10,11... | collective-permute-start | bytes 3145736 | tf_op jit(solution)/shard_map/ppermute | solution.py:383
  278.4 129.4 %collective-permute-start.24 = (bf16[2,2,128,1024]{3,2,1,0:T(8,128)(2,1)}, bf16[2,2,128,1024]{3,2,1,0:T(8,128)(2,1)}, u32[]{:S(2)}, u32[]{:S(2)}) collective-permute-start(bf16[2,2,128,1024]{3,2,1,0:T(8,128)(2,1)} %collective-permute-done.23.refs_36_), channel_id=1, source_target_pairs={{0,1},{1,0},{2,3},{3,2},{4,5},{5,4},{6,7},{7,6},{8,9},{9,8},{10,11... | collective-permute-start | bytes 3145736 | tf_op jit(solution)/shard_map/ppermute | solution.py:383
  320.6 87.2 %collective-permute-start.26 = (bf16[2,2,128,1024]{3,2,1,0:T(8,128)(2,1)}, bf16[2,2,128,1024]{3,2,1,0:T(8,128)(2,1)}, u32[]{:S(2)}, u32[]{:S(2)}) collective-permute-start(bf16[2,2,128,1024]{3,2,1,0:T(8,128)(2,1)} %collective-permute-done.25.refs_38_), channel_id=1, source_target_pairs={{0,1},{1,0},{2,3},{3,2},{4,5},{5,4},{6,7},{7,6},{8,9},{9,8},{10,11... | collective-permute-start | bytes 3145736 | tf_op jit(solution)/shard_map/ppermute | solution.py:383
  423.4 35.7 %all-to-all-start = ((f32[32,8,128]{2,1,0:T(8,128)}), f32[32,8,128]{2,1,0:T(8,128)S(1)}, u32[]{:S(2)}, u32[]{:S(2)}) async-start(f32[32,8,128]{2,1,0:T(8,128)} %broadcast_in_dim.27), calls=%async_computation | async-start | bytes 262144 | tf_op jit(solution)/shard_map/all_to_all | solution.py:449
  (21 other events, 281.7 us)

commit v2 on v1

--- a/solution.py
+++ b/solution.py
@@ -240,7 +240,7 @@
         lax.fori_loop(0, nev // group, y_step, 0)
 
 
-def modes(nev, tsrc, info, own, came, mats):
+def modes(nev, tsrc, info, own, came, mats, room):
     held = len(came)
     lines, width = came[0].shape[1:]
     steps = lines // ROWS
@@ -259,12 +259,12 @@
             pltpu.VMEM((2, nev * PITCH, nev), jnp.float32),
             pltpu.SemaphoreType.DMA((2,)),
         ],
-        compiler_params=pltpu.CompilerParams(vmem_limit_bytes=48 << 20),
+        compiler_params=pltpu.CompilerParams(vmem_limit_bytes=room << 20),
         name="modes",
     )(info, own, *came, mats)
 
 
-def inner_kernel(nev, tsrc, slots, counts, groups, begin, where_ref, *refs):
+def inner_kernel(nev, tsrc, slots, counts, groups, begin, final, where_ref, *refs):
     refs = list(refs)
 
     def take(count):
@@ -316,9 +316,15 @@
                 c_im = jnp.sum(f_re * m_im + f_im * m_re, axis=0, keepdims=True)
                 out_ref[at : at + 1, :] = before_ref[at : at + 1, :] + c_re
                 out_ref[at + 1 : at + 2, :] = before_ref[at + 1 : at + 2, :] + c_im
-
-
-def inner_products(nev, tsrc, ys, begin, groups, sources, where, mats, before):
+        if final:
+            sums = jnp.sum(out_ref[...], axis=1, keepdims=True)
+            row = lax.broadcasted_iota(jnp.int32, out_ref.shape, 0)
+            lane = lax.broadcasted_iota(jnp.int32, out_ref.shape, 1)
+            placed = jnp.sum(jnp.where(row == lane, sums, 0.0), axis=0, keepdims=True)
+            out_ref[...] = jnp.broadcast_to(placed, out_ref.shape)
+
+
+def inner_products(nev, tsrc, ys, begin, groups, sources, where, mats, before, final):
     slots = ys[0].shape[0]
     counts = [piece.shape[3] for piece in ys]
     lines = sum(counts)
@@ -343,7 +349,7 @@
     specs.append(pl.BlockSpec((slots, tsrc * nev, 2 * nev), lambda s, w: (0, 4, 0)))
     specs.append(pl.BlockSpec(before.shape, lambda s, w: (0, 0)))
     return pl.pallas_call(
-        functools.partial(inner_kernel, nev, tsrc, slots, counts, groups, begin),
+        functools.partial(inner_kernel, nev, tsrc, slots, counts, groups, begin, final),
         out_shape=jax.ShapeDtypeStruct(before.shape, jnp.float32),
         grid_spec=pltpu.PrefetchScalarGridSpec(
             num_scalar_prefetch=1,
@@ -423,7 +429,7 @@
     ys = []
     for h in range(len(sizes)):
         info = jnp.stack([stays.astype(jnp.int32), t % held * nev + begins[h]]).astype(jnp.int32)
-        ys.append(modes(nev, tsrc, info, sink, arrived[h], mats))
+        ys.append(modes(nev, tsrc, info, sink, arrived[h], mats, 48 if h < len(sizes) - 2 else 63))
 
     total = jnp.zeros((held * tsrc * 2, nev), jnp.float32)
     places = {}
@@ -443,11 +449,12 @@
             jnp.stack([at for n in names for at in places[n]]).astype(jnp.int32),
             mats,
             total,
+            name == "last",
         )
 
-    spread = jnp.broadcast_to(total[None], (times * depth, *total.shape))
+    spread = jnp.broadcast_to(total[:1][None], (times * depth, 1, nev))
     spread = lax.all_to_all(spread, AXES, 0, 0, tiled=True)
-    values = jnp.sum(spread, axis=-1).reshape(times, chips, CORES, held, tsrc, 2)
+    values = spread[:, 0, : held * tsrc * 2].reshape(times, chips, CORES, held, tsrc, 2)
     slot_of = (jnp.arange(times) - t) % held
     pick = (jnp.arange(held)[None, None] == slot_of[:, None, None]) & (
         jnp.arange(CORES)[None, :, None] == t // held

time: 461 us -> 466 us (1.011)
    unnamed x36 -> x42, local copies, waits for them, and re-layouts: 8.34 us -> 11.4 us
where the time goes in v2:
time: 466 us; the launch traced here: 465 us
  waiting for transfers between devices  163 us (35%)
  starting transfers between devices  159 us (34%)
  Pallas kernels  97.7 us (21%)
  local copies, waits for them, and re-layouts  39 us (8%)
    ppermute x27, waiting for transfers between devices, move(): return lax.ppermute(value, AXES, pairs)  155 us
    ppermute x27, starting transfers between devices, move(): return lax.ppermute(value, AXES, pairs)  131 us
    pallas_call x5, Pallas kernels, modes(): pl.pallas_call(functools.partial(mode_kernel, nev, tsrc, held, 64), out_s...  52.6 us
    pallas_call x4, Pallas kernels, inner_products(): pl.pallas_call(functools.partial(inner_kernel, nev, tsrc, slots, counts,...  42.9 us
    all_to_all x1, starting transfers between devices, chip_plan(): spread = lax.all_to_all(spread, AXES, 0, 0, tiled=True)  28.2 us
    dynamic_slice x3, local copies, waits for them, and re-layouts, send(): lax.dynamic_slice(after, (0, line, 0), (2, sizes[h], after.shape[2]))  12.9 us
    unnamed x42, local copies, waits for them, and re-layouts  11.4 us
  transfers between devices with their start and end apart: 28, of which 7 were waited for; matrix products, arithmetic and copies ran while one was open for 6% of the time, Pallas kernels for 18%

profile of v2, /device:TPU:0, one launch (start us, length us, event | category | flops | bytes accessed | tf_op | source)
XLA Modules:
  0.0 465.0 jit_solution(10522571533784605185)
XLA Ops:
  0.0 5.1 %collective-permute-start.2 = (bf16[2,2,64,512]{3,2,1,0:T(8,128)(2,1)}, bf16[2,2,64,512]{3,2,1,0:T(8,128)(2,1)S(1)}, u32[]{:S(2)}, u32[]{:S(2)}) collective-permute-start(bf16[2,2,64,512]{3,2,1,0:T(8,128)(2,1)} %bitcast.49), channel_id=1, source_target_pairs={{0,6},{1,7},{2,0},{3,1},{4,2},{5,3},{6,4},{7,5},{8,14},{9,15},{10,... | collective-permute-start | bytes 786440 | tf_op jit(solution)/shard_map/ppermute | solution.py:389
  8.8 4.3 constant_dynamic-slice_fusion
  17.9 33.4 %collective-permute-done.1 = bf16[2,2,64,512]{3,2,1,0:T(8,128)(2,1)S(1)} collective-permute-done((bf16[2,2,64,512]{3,2,1,0:T(8,128)(2,1)}, bf16[2,2,64,512]{3,2,1,0:T(8,128)(2,1)S(1)}, u32[]{:S(2)}, u32[]{:S(2)}) %collective-permute-start.1) | collective-permute-done | bytes 262176 | tf_op jit(solution)/shard_map/ppermute | solution.py:389
  55.7 40.6 %collective-permute-done.19.refs_24_.refs_32_ = bf16[2,2,128,1024]{3,2,1,0:T(8,128)(2,1)} collective-permute-done((bf16[2,2,128,1024]{3,2,1,0:T(8,128)(2,1)}, bf16[2,2,128,1024]{3,2,1,0:T(8,128)(2,1)}, u32[]{:S(2)}, u32[]{:S(2)}) %collective-permute-start.19) | collective-permute-done | bytes 1048608 | tf_op jit(solution)/shard_map/ppermute | solution.py:389
  99.4 41.8 %collective-permute-done.23.refs_36_ = bf16[2,2,128,1024]{3,2,1,0:T(8,128)(2,1)} collective-permute-done((bf16[2,2,128,1024]{3,2,1,0:T(8,128)(2,1)}, bf16[2,2,128,1024]{3,2,1,0:T(8,128)(2,1)}, u32[]{:S(2)}, u32[]{:S(2)}) %collective-permute-start.23) | collective-permute-done | bytes 1048608 | tf_op jit(solution)/shard_map/ppermute | solution.py:389
  144.4 4.7 %dynamic-slice_bitcast_fusion = (bf16[2,32,16384]{2,1,0:T(8,128)(2,1)}, bf16[2,32,16384]{2,1,0:T(8,128)(2,1)}) fusion(bf16[2,1,256,16384]{3,2,1,0:T(8,128)(2,1)} %param.5, s32[]{:T(128)S(6)} %select_n.193, s32[]{:T(128)S(6)} %select_n.192), kind=kLoop, calls=%fused_computation | loop fusion | bytes 8388616 | tf_op jit(solution)/shard_map/dynamic_slice | solution.py:406
  152.7 4.8 %constant_dynamic-slice_fusion.6 = (bf16[2,2,128,2048]{3,2,1,0:T(8,128)(2,1)}, bf16[2,2,128,2048]{3,2,1,0:T(8,128)(2,1)}) fusion(bf16[2,2,2048,2048]{3,2,1,0:T(8,128)(2,1)} %param.6, s32[]{:T(128)S(6)} %select_n.204, s32[]{:T(128)S(6)} %select_n.201), kind=kLoop, calls=%fused_computation.11 | loop fusion | bytes 8388616 | tf_op jit(solution)/shard_map/dynamic_slice | solution.py:415
  159.0 7.9 %collective-permute-start.16 = (bf16[2,2,128,2048]{3,2,1,0:T(8,128)(2,1)}, bf16[2,2,128,2048]{3,2,1,0:T(8,128)(2,1)}, u32[]{:S(2)}, u32[]{:S(2)}) collective-permute-start(bf16[2,2,128,2048]{3,2,1,0:T(8,128)(2,1)} %get-tuple-element.16.refs_8_.refs_4_.refs_20_.refs_28_), channel_id=1, source_target_pairs={{0,1},{1,0},{2,3},{3,2},{4,5},{5,4},{6,7},{7,6},{8,9},{9,8},{10,11... | collective-permute-start | bytes 6291464 | tf_op jit(solution)/shard_map/ppermute | solution.py:389
  168.5 22.9 %collective-permute-start.17 = (bf16[2,2,128,2048]{3,2,1,0:T(8,128)(2,1)}, bf16[2,2,128,2048]{3,2,1,0:T(8,128)(2,1)}, u32[]{:S(2)}, u32[]{:S(2)}) collective-permute-start(bf16[2,2,128,2048]{3,2,1,0:T(8,128)(2,1)} %get-tuple-element.15), channel_id=1, source_target_pairs={{0,2},{1,3},{2,4},{3,5},{4,6},{5,7},{6,0},{7,1},{8,10},{9,11},{10,... | collective-permute-start | bytes 6291464 | tf_op jit(solution)/shard_map/ppermute | solution.py:389
  197.0 24.8 %collective-permute-done.7.refs_3_ = bf16[768,256]{1,0:T(8,128)(2,1)S(1)} collective-permute-done((bf16[768,256]{1,0:T(8,128)(2,1)S(1)}, bf16[768,256]{1,0:T(8,128)(2,1)S(1)}, u32[]{:S(2)}, u32[]{:S(2)}) %collective-permute-start.7) | collective-permute-done | bytes 393248 | tf_op jit(solution)/shard_map/ppermute | solution.py:389
  226.3 13.2 %collective-permute-done.17.refs_10_.refs_6_.refs_22_.refs_30_ = bf16[2,2,128,2048]{3,2,1,0:T(8,128)(2,1)} collective-permute-done((bf16[2,2,128,2048]{3,2,1,0:T(8,128)(2,1)}, bf16[2,2,128,2048]{3,2,1,0:T(8,128)(2,1)}, u32[]{:S(2)}, u32[]{:S(2)}) %collective-permute-start.17) | collective-permute-done | bytes 2097184 | tf_op jit(solution)/shard_map/ppermute | solution.py:389
  242.3 30.1 %collective-permute-start.20 = (bf16[2,2,128,1024]{3,2,1,0:T(8,128)(2,1)}, bf16[2,2,128,1024]{3,2,1,0:T(8,128)(2,1)}, u32[]{:S(2)}, u32[]{:S(2)}) collective-permute-start(bf16[2,2,128,1024]{3,2,1,0:T(8,128)(2,1)} %collective-permute-done.19.refs_24_.refs_32_), channel_id=1, source_target_pairs={{0,1},{1,0},{2,3},{3,2},{4,5},{5,4},{6,7},{7,6},{8,9},{9,8},{10,11... | collective-permute-start | bytes 3145736 | tf_op jit(solution)/shard_map/ppermute | solution.py:389
  278.3 40.9 %collective-permute-start.24 = (bf16[2,2,128,1024]{3,2,1,0:T(8,128)(2,1)}, bf16[2,2,128,1024]{3,2,1,0:T(8,128)(2,1)}, u32[]{:S(2)}, u32[]{:S(2)}) collective-permute-start(bf16[2,2,128,1024]{3,2,1,0:T(8,128)(2,1)} %collective-permute-done.23.refs_36_), channel_id=1, source_target_pairs={{0,1},{1,0},{2,3},{3,2},{4,5},{5,4},{6,7},{7,6},{8,9},{9,8},{10,11... | collective-permute-start | bytes 3145736 | tf_op jit(solution)/shard_map/ppermute | solution.py:389
  328.0 8.1 %modes.5.refs_0_.refs_1_.refs_2_.refs_3_.refs_4_.refs_5_.refs_6_.refs_7_.refs_12_.refs_17_.refs_22_.refs_27_ = bf16[2,2,2,16,16384]{4,3,2,1,0:T(8,128)(2,1)} custom-call(s32[2]{0:T(128)} %get-tuple-element.31.info_ref, bf16[2,256,16384]{2,1,0:T(8,128)(2,1)} %bitcast.44, bf16[2,16,16384]{2,1,0:T(8,128)(2,1)} %collective-permute-done.3.refs_0_, ...), custom_call_target="tpu_custom_call" | custom-call | tf_op jit(solution)/shard_map/modes/pallas_call | solution.py:248
  336.1 8.0 %modes.9.refs_0_.refs_1_.refs_2_.refs_3_.refs_7_.refs_11_.refs_15_.refs_19_.refs_16_.refs_21_.refs_26_ = bf16[2,2,2,16,16384]{4,3,2,1,0:T(8,128)(2,1)} custom-call(s32[2]{0:T(128)} %pad_add_fusion.5.info_ref, bf16[2,256,16384]{2,1,0:T(8,128)(2,1)} %bitcast.45, bf16[2,16,16384]{2,1,0:T(8,128)(2,1)} %collective-permute-done.14.refs_0_, ...), custom_call_target="tpu_custom_call" | custom-call | tf_op jit(solution)/shard_map/modes/pallas_call | solution.py:248
  347.0 12.2 %modes.6.refs_0_.refs_2_.refs_4_.refs_6_.refs_8_.refs_12_.refs_16_.refs_13_.refs_18_.refs_23_ = bf16[2,2,2,32,16384]{4,3,2,1,0:T(8,128)(2,1)} custom-call(s32[2]{0:T(128)S(1)} %get-tuple-element.32.info_ref, bf16[2,256,16384]{2,1,0:T(8,128)(2,1)} %bitcast.46, bf16[2,32,16384]{2,1,0:T(8,128)(2,1)S(1)} %copy-done.4, ...), custom_call_target="tpu_custom_call" | custom-call | tf_op jit(solution)/shard_map/modes/pallas_call | solution.py:248
  359.3 12.3 %modes.7.refs_1_.refs_3_.refs_5_.refs_7_.refs_9_.refs_13_.refs_17_.refs_14_.refs_19_.refs_24_ = bf16[2,2,2,32,16384]{4,3,2,1,0:T(8,128)(2,1)} custom-call(s32[2]{0:T(128)S(1)} %get-tuple-element.33.info_ref, bf16[2,256,16384]{2,1,0:T(8,128)(2,1)} %bitcast.47, bf16[2,32,16384]{2,1,0:T(8,128)(2,1)S(1)} %copy-done.6, bf16[2,32,16384]{2,1,0:T(8,128)(2,1)S(1)} %copy-done.8, ...), custom_call_target="tpu_custom_call" | custom-call | tf_op jit(solution)/shard_map/modes/pallas_call | solution.py:248
  371.6 12.0 %modes.8.refs_0_.refs_1_.refs_2_.refs_3_.refs_6_.refs_10_.refs_14_.refs_18_.refs_15_.refs_20_.refs_25_ = bf16[2,2,2,32,16384]{4,3,2,1,0:T(8,128)(2,1)} custom-call(s32[2]{0:T(128)S(1)} %get-tuple-element.34.info_ref, bf16[2,256,16384]{2,1,0:T(8,128)(2,1)} %bitcast.48, bf16[2,32,16384]{2,1,0:T(8,128)(2,1)S(1)} %copy-done.10, ...), custom_call_target="tpu_custom_call" | custom-call | tf_op jit(solution)/shard_map/modes/pallas_call | solution.py:248
  384.2 8.9 %inner.4.refs_9_ = f32[8,128]{1,0:T(8,128)} custom-call(s32[4]{0:T(128)} %pad_add_fusion.6.where_ref, bf16[2,2,2,32,16384]{4,3,2,1,0:T(8,128)(2,1)} %modes.6.refs_0_.refs_2_.refs_4_.refs_6_.refs_8_.refs_12_.refs_16_.refs_13_.refs_18_.refs_23_, ...), custom_call_target="tpu_custom_call" | custom-call | tf_op jit(solution)/shard_map/inner/pallas_call | solution.py:351
  393.1 8.0 %inner.5.refs_29_ = f32[8,128]{1,0:T(8,128)} custom-call(s32[4]{0:T(128)} %pad_add_fusion.6.where_ref, bf16[2,2,2,32,16384]{4,3,2,1,0:T(8,128)(2,1)} %modes.8.refs_0_.refs_1_.refs_2_.refs_3_.refs_6_.refs_10_.refs_14_.refs_18_.refs_15_.refs_20_.refs_25_, ...), custom_call_target="tpu_custom_call" | custom-call | tf_op jit(solution)/shard_map/inner/pallas_call | solution.py:351
  401.1 11.8 %inner.6.refs_41_ = f32[8,128]{1,0:T(8,128)} custom-call(s32[8]{0:T(128)} %stack.158.where_ref, bf16[2,2,2,16,16384]{4,3,2,1,0:T(8,128)(2,1)} %modes.9.refs_0_.refs_1_.refs_2_.refs_3_.refs_7_.refs_11_.refs_15_.refs_19_.refs_16_.refs_21_.refs_26_, ...), custom_call_target="tpu_custom_call" | custom-call | tf_op jit(solution)/shard_map/inner/pallas_call | solution.py:351
  412.9 14.3 %inner.7 = f32[8,128]{1,0:T(8,128)} custom-call(s32[12]{0:T(128)} %stack.138.where_ref, bf16[2,2,2,16,16384]{4,3,2,1,0:T(8,128)(2,1)} %modes.5.refs_0_.refs_1_.refs_2_.refs_3_.refs_4_.refs_5_.refs_6_.refs_7_.refs_12_.refs_17_.refs_22_.refs_27_, ...), custom_call_target="tpu_custom_call" | custom-call | tf_op jit(solution)/shard_map/inner/pallas_call | solution.py:351
  428.5 28.2 %all-to-all-start = ((f32[32,1,128]{2,1,0:T(1,128)}), f32[32,1,128]{2,1,0:T(1,128)S(1)}, u32[]{:S(2)}, u32[]{:S(2)}) async-start(f32[32,1,128]{2,1,0:T(1,128)} %broadcast_in_dim.30), calls=%async_computation | async-start | bytes 32768 | tf_op jit(solution)/shard_map/all_to_all | solution.py:456
  456.8 7.1 %all-to-all-done = f32[32,1,128]{2,1,0:T(1,128)S(1)} async-done(((f32[32,1,128]{2,1,0:T(1,128)}), f32[32,1,128]{2,1,0:T(1,128)S(1)}, u32[]{:S(2)}, u32[]{:S(2)}) %all-to-all-start) | async-done | bytes 16416 | tf_op jit(solution)/shard_map/all_to_all | solution.py:456
  (112 shorter events, 56.9 us)
Async XLA Ops:
  5.1 46.2 %collective-permute-start.1 = (bf16[2,2,64,512]{3,2,1,0:T(8,128)(2,1)}, bf16[2,2,64,512]{3,2,1,0:T(8,128)(2,1)S(1)}, u32[]{:S(2)}, u32[]{:S(2)}) collective-permute-start(bf16[2,2,64,512]{3,2,1,0:T(8,128)(2,1)} %bitcast.50), channel_id=1, source_target_pairs={{0,4},{1,5},{2,6},{3,7},{4,0},{5,1},{6,2},{7,3},{8,12},{9,13},{10,... | collective-permute-start | bytes 786440 | tf_op jit(solution)/shard_map/ppermute | solution.py:389
  5.1 46.2 %collective-permute-start = (bf16[2,2,64,512]{3,2,1,0:T(8,128)(2,1)}, bf16[2,2,64,512]{3,2,1,0:T(8,128)(2,1)S(1)}, u32[]{:S(2)}, u32[]{:S(2)}) collective-permute-start(bf16[2,2,64,512]{3,2,1,0:T(8,128)(2,1)} %bitcast.51), channel_id=1, source_target_pairs={{0,2},{1,3},{2,4},{3,5},{4,6},{5,7},{6,0},{7,1},{8,10},{9,11},{10,... | collective-permute-start | bytes 786440 | tf_op jit(solution)/shard_map/ppermute | solution.py:389
  13.0 83.3 %collective-permute-start.19 = (bf16[2,2,128,1024]{3,2,1,0:T(8,128)(2,1)}, bf16[2,2,128,1024]{3,2,1,0:T(8,128)(2,1)}, u32[]{:S(2)}, u32[]{:S(2)}) collective-permute-start(bf16[2,2,128,1024]{3,2,1,0:T(8,128)(2,1)} %get-tuple-element.13), channel_id=1, source_target_pairs={{0,4},{1,5},{2,6},{3,7},{4,0},{5,1},{6,2},{7,3},{8,12},{9,13},{10,... | collective-permute-start | bytes 3145736 | tf_op jit(solution)/shard_map/ppermute | solution.py:389
  14.9 83.0 %collective-permute-start.21 = (bf16[2,2,128,1024]{3,2,1,0:T(8,128)(2,1)}, bf16[2,2,128,1024]{3,2,1,0:T(8,128)(2,1)}, u32[]{:S(2)}, u32[]{:S(2)}) collective-permute-start(bf16[2,2,128,1024]{3,2,1,0:T(8,128)(2,1)} %get-tuple-element.12), channel_id=1, source_target_pairs={{0,6},{1,7},{2,0},{3,1},{4,2},{5,3},{6,4},{7,5},{8,14},{9,15},{10,... | collective-permute-start | bytes 3145736 | tf_op jit(solution)/shard_map/ppermute | solution.py:389
  17.9 123.4 %collective-permute-start.23 = (bf16[2,2,128,1024]{3,2,1,0:T(8,128)(2,1)}, bf16[2,2,128,1024]{3,2,1,0:T(8,128)(2,1)}, u32[]{:S(2)}, u32[]{:S(2)}) collective-permute-start(bf16[2,2,128,1024]{3,2,1,0:T(8,128)(2,1)} %get-tuple-element.14), channel_id=1, source_target_pairs={{0,4},{1,5},{2,6},{3,7},{4,0},{5,1},{6,2},{7,3},{8,12},{9,13},{10,... | collective-permute-start | bytes 3145736 | tf_op jit(solution)/shard_map/ppermute | solution.py:389
  51.2 100.8 %collective-permute-start.25 = (bf16[2,2,128,1024]{3,2,1,0:T(8,128)(2,1)}, bf16[2,2,128,1024]{3,2,1,0:T(8,128)(2,1)}, u32[]{:S(2)}, u32[]{:S(2)}) collective-permute-start(bf16[2,2,128,1024]{3,2,1,0:T(8,128)(2,1)} %get-tuple-element.11), channel_id=1, source_target_pairs={{0,6},{1,7},{2,0},{3,1},{4,2},{5,3},{6,4},{7,5},{8,14},{9,15},{10,... | collective-permute-start | bytes 3145736 | tf_op jit(solution)/shard_map/ppermute | solution.py:389
  51.4 91.5 %collective-permute-start.5 = (bf16[4,2,2,64,512]{4,3,2,1,0:T(8,128)(2,1)S(1)}, bf16[4,2,2,64,512]{4,3,2,1,0:T(8,128)(2,1)S(1)}, u32[]{:S(2)}, u32[]{:S(2)}) collective-permute-start(bf16[4,2,2,64,512]{4,3,2,1,0:T(8,128)(2,1)S(1)} %pad_maximum_fusion.mine_ref), channel_id=1, source_target_pairs={{0,1},{1,0},{2,3},{3,2},{4,5},{5,4},{6,7},{7,6},{8,9},{9,8},{10,11... | collective-permute-start | bytes 3145736 | tf_op jit(solution)/shard_map/ppermute | solution.py:389
  96.3 61.2 %collective-permute-start.3 = (bf16[2,16,16384]{2,1,0:T(8,128)(2,1)}, bf16[2,16,16384]{2,1,0:T(8,128)(2,1)}, u32[]{:S(2)}, u32[]{:S(2)}) collective-permute-start(bf16[2,16,16384]{2,1,0:T(8,128)(2,1)} %get-tuple-element.20), channel_id=1, source_target_pairs={{1,16},{3,18},{5,20},{7,22},{9,24},{11,26},{13,28},{15,30},{16,1},... | collective-permute-start | bytes 3145736 | tf_op jit(solution)/shard_map/ppermute | solution.py:389
  98.0 60.4 %collective-permute-start.4 = (bf16[2,16,16384]{2,1,0:T(8,128)(2,1)}, bf16[2,16,16384]{2,1,0:T(8,128)(2,1)}, u32[]{:S(2)}, u32[]{:S(2)}) collective-permute-start(bf16[2,16,16384]{2,1,0:T(8,128)(2,1)} %get-tuple-element.19), channel_id=1, source_target_pairs={{0,8},{1,24},{2,10},{3,26},{4,12},{5,28},{6,14},{7,30},{8,0},{9,16... | collective-permute-start | bytes 3145736 | tf_op jit(solution)/shard_map/ppermute | solution.py:389
  152.0 39.4 %collective-permute-start.6 = (bf16[768,256]{1,0:T(8,128)(2,1)S(1)}, bf16[768,256]{1,0:T(8,128)(2,1)S(1)}, u32[]{:S(2)}, u32[]{:S(2)}) collective-permute-start(bf16[768,256]{1,0:T(8,128)(2,1)S(1)} %get-tuple-element.9.refs_0_), channel_id=1, source_target_pairs={{1,16},{3,18},{5,20},{7,22},{9,24},{11,26},{13,28},{15,30},{16,1},... | collective-permute-start | bytes 1179656 | tf_op jit(solution)/shard_map/ppermute | solution.py:389
  157.6 65.8 %collective-permute-start.8 = (bf16[2,32,16384]{2,1,0:T(8,128)(2,1)}, bf16[2,32,16384]{2,1,0:T(8,128)(2,1)S(1)}, u32[]{:S(2)}, u32[]{:S(2)}) collective-permute-start(bf16[2,32,16384]{2,1,0:T(8,128)(2,1)} %get-tuple-element.26), channel_id=1, source_target_pairs={{1,16},{3,18},{5,20},{7,22},{9,24},{11,26},{13,28},{15,30},{16,1},... | collective-permute-start | bytes 6291464 | tf_op jit(solution)/shard_map/ppermute | solution.py:389
  158.4 66.6 %collective-permute-start.9 = (bf16[2,32,16384]{2,1,0:T(8,128)(2,1)}, bf16[2,32,16384]{2,1,0:T(8,128)(2,1)}, u32[]{:S(2)}, u32[]{:S(2)}) collective-permute-start(bf16[2,32,16384]{2,1,0:T(8,128)(2,1)} %get-tuple-element.25), channel_id=1, source_target_pairs={{0,8},{1,24},{2,10},{3,26},{4,12},{5,28},{6,14},{7,30},{8,0},{9,16... | collective-permute-start | bytes 6291464 | tf_op jit(solution)/shard_map/ppermute | solution.py:389
  159.0 66.8 %collective-permute-start.16 = (bf16[2,2,128,2048]{3,2,1,0:T(8,128)(2,1)}, bf16[2,2,128,2048]{3,2,1,0:T(8,128)(2,1)}, u32[]{:S(2)}, u32[]{:S(2)}) collective-permute-start(bf16[2,2,128,2048]{3,2,1,0:T(8,128)(2,1)} %get-tuple-element.16.refs_8_.refs_4_.refs_20_.refs_28_), channel_id=1, source_target_pairs={{0,1},{1,0},{2,3},{3,2},{4,5},{5,4},{6,7},{7,6},{8,9},{9,8},{10,11... | collective-permute-start | bytes 6291464 | tf_op jit(solution)/shard_map/ppermute | solution.py:389
  168.5 70.9 %collective-permute-start.17 = (bf16[2,2,128,2048]{3,2,1,0:T(8,128)(2,1)}, bf16[2,2,128,2048]{3,2,1,0:T(8,128)(2,1)}, u32[]{:S(2)}, u32[]{:S(2)}) collective-permute-start(bf16[2,2,128,2048]{3,2,1,0:T(8,128)(2,1)} %get-tuple-element.15), channel_id=1, source_target_pairs={{0,2},{1,3},{2,4},{3,5},{4,6},{5,7},{6,0},{7,1},{8,10},{9,11},{10,... | collective-permute-start | bytes 6291464 | tf_op jit(solution)/shard_map/ppermute | solution.py:389
  191.4 30.3 %collective-permute-start.7 = (bf16[768,256]{1,0:T(8,128)(2,1)S(1)}, bf16[768,256]{1,0:T(8,128)(2,1)S(1)}, u32[]{:S(2)}, u32[]{:S(2)}) collective-permute-start(bf16[768,256]{1,0:T(8,128)(2,1)S(1)} %get-tuple-element.10.refs_1_), channel_id=1, source_target_pairs={{0,8},{1,24},{2,10},{3,26},{4,12},{5,28},{6,14},{7,30},{8,0},{9,16... | collective-permute-start | bytes 1179656 | tf_op jit(solution)/shard_map/ppermute | solution.py:389
  223.3 49.1 %collective-permute-start.11 = (bf16[2,32,16384]{2,1,0:T(8,128)(2,1)S(1)}, bf16[2,32,16384]{2,1,0:T(8,128)(2,1)S(1)}, u32[]{:S(2)}, u32[]{:S(2)}) collective-permute-start(bf16[2,32,16384]{2,1,0:T(8,128)(2,1)S(1)} %get-tuple-element.23), channel_id=1, source_target_pairs={{0,8},{1,24},{2,10},{3,26},{4,12},{5,28},{6,14},{7,30},{8,0},{9,16... | collective-permute-start | bytes 6291464 | tf_op jit(solution)/shard_map/ppermute | solution.py:389
  224.9 52.1 %collective-permute-start.12 = (bf16[2,32,16384]{2,1,0:T(8,128)(2,1)S(1)}, bf16[2,32,16384]{2,1,0:T(8,128)(2,1)S(1)}, u32[]{:S(2)}, u32[]{:S(2)}) collective-permute-start(bf16[2,32,16384]{2,1,0:T(8,128)(2,1)S(1)} %get-tuple-element.22), channel_id=1, source_target_pairs={{1,16},{3,18},{5,20},{7,22},{9,24},{11,26},{13,28},{15,30},{16,1},... | collective-permute-start | bytes 6291464 | tf_op jit(solution)/shard_map/ppermute | solution.py:389
  225.7 93.5 %collective-permute-start.13 = (bf16[2,32,16384]{2,1,0:T(8,128)(2,1)S(1)}, bf16[2,32,16384]{2,1,0:T(8,128)(2,1)S(1)}, u32[]{:S(2)}, u32[]{:S(2)}) collective-permute-start(bf16[2,32,16384]{2,1,0:T(8,128)(2,1)S(1)} %get-tuple-element.21), channel_id=1, source_target_pairs={{0,8},{1,24},{2,10},{3,26},{4,12},{5,28},{6,14},{7,30},{8,0},{9,16... | collective-permute-start | bytes 6291464 | tf_op jit(solution)/shard_map/ppermute | solution.py:389
  239.5 144.2 %collective-permute-start.18 = (bf16[2,2,128,2048]{3,2,1,0:T(8,128)(2,1)}, bf16[2,2,128,2048]{3,2,1,0:T(8,128)(2,1)}, u32[]{:S(2)}, u32[]{:S(2)}) collective-permute-start(bf16[2,2,128,2048]{3,2,1,0:T(8,128)(2,1)} %collective-permute-done.17.refs_10_.refs_6_.refs_22_.refs_30_), channel_id=1, source_target_pairs={{0,1},{1,0},{2,3},{3,2},{4,5},{5,4},{6,7},{7,6},{8,9},{9,8},{10,11... | collective-permute-start | bytes 6291464 | tf_op jit(solution)/shard_map/ppermute | solution.py:389
  242.3 158.8 %collective-permute-start.20 = (bf16[2,2,128,1024]{3,2,1,0:T(8,128)(2,1)}, bf16[2,2,128,1024]{3,2,1,0:T(8,128)(2,1)}, u32[]{:S(2)}, u32[]{:S(2)}) collective-permute-start(bf16[2,2,128,1024]{3,2,1,0:T(8,128)(2,1)} %collective-permute-done.19.refs_24_.refs_32_), channel_id=1, source_target_pairs={{0,1},{1,0},{2,3},{3,2},{4,5},{5,4},{6,7},{7,6},{8,9},{9,8},{10,11... | collective-permute-start | bytes 3145736 | tf_op jit(solution)/shard_map/ppermute | solution.py:389
  273.7 127.4 %collective-permute-start.22 = (bf16[2,2,128,1024]{3,2,1,0:T(8,128)(2,1)}, bf16[2,2,128,1024]{3,2,1,0:T(8,128)(2,1)}, u32[]{:S(2)}, u32[]{:S(2)}) collective-permute-start(bf16[2,2,128,1024]{3,2,1,0:T(8,128)(2,1)} %collective-permute-done.21.refs_26_.refs_34_), channel_id=1, source_target_pairs={{0,1},{1,0},{2,3},{3,2},{4,5},{5,4},{6,7},{7,6},{8,9},{9,8},{10,11... | collective-permute-start | bytes 3145736 | tf_op jit(solution)/shard_map/ppermute | solution.py:389
  278.3 134.6 %collective-permute-start.24 = (bf16[2,2,128,1024]{3,2,1,0:T(8,128)(2,1)}, bf16[2,2,128,1024]{3,2,1,0:T(8,128)(2,1)}, u32[]{:S(2)}, u32[]{:S(2)}) collective-permute-start(bf16[2,2,128,1024]{3,2,1,0:T(8,128)(2,1)} %collective-permute-done.23.refs_36_), channel_id=1, source_target_pairs={{0,1},{1,0},{2,3},{3,2},{4,5},{5,4},{6,7},{7,6},{8,9},{9,8},{10,11... | collective-permute-start | bytes 3145736 | tf_op jit(solution)/shard_map/ppermute | solution.py:389
  320.6 92.3 %collective-permute-start.26 = (bf16[2,2,128,1024]{3,2,1,0:T(8,128)(2,1)}, bf16[2,2,128,1024]{3,2,1,0:T(8,128)(2,1)}, u32[]{:S(2)}, u32[]{:S(2)}) collective-permute-start(bf16[2,2,128,1024]{3,2,1,0:T(8,128)(2,1)} %collective-permute-done.25.refs_38_), channel_id=1, source_target_pairs={{0,1},{1,0},{2,3},{3,2},{4,5},{5,4},{6,7},{7,6},{8,9},{9,8},{10,11... | collective-permute-start | bytes 3145736 | tf_op jit(solution)/shard_map/ppermute | solution.py:389
  428.5 35.4 %all-to-all-start = ((f32[32,1,128]{2,1,0:T(1,128)}), f32[32,1,128]{2,1,0:T(1,128)S(1)}, u32[]{:S(2)}, u32[]{:S(2)}) async-start(f32[32,1,128]{2,1,0:T(1,128)} %broadcast_in_dim.30), calls=%async_computation | async-start | bytes 32768 | tf_op jit(solution)/shard_map/all_to_all | solution.py:456
  (24 other events, 399.3 us)

commit v3 on v2

--- a/solution.py
+++ b/solution.py
@@ -251,12 +251,12 @@
         grid=(held * steps,),
         in_specs=[pl.BlockSpec(memory_space=pltpu.SMEM), hbm]
         + [hbm] * held
-        + [pl.BlockSpec((1, *mats.shape[1:]), lambda g: (g // steps, 0, 0))],
+        + [pl.BlockSpec((1, tsrc * 4 * nev, 2 * nev), lambda g: (g // steps, 0, 0))],
         out_specs=pl.BlockSpec((1, tsrc, 2, ROWS, width), lambda g: (g // steps, 0, 0, g % steps, 0)),
         scratch_shapes=[
             pltpu.VMEM((2, 2, ROWS, width), jnp.bfloat16),
-            pltpu.VMEM((2 * tsrc, nev * PITCH, nev), jnp.float32),
-            pltpu.VMEM((2, nev * PITCH, nev), jnp.float32),
+            pltpu.VMEM((2 * tsrc, (nev + 2) * PITCH, nev), jnp.float32),
+            pltpu.VMEM((2, (nev + 2) * PITCH, nev), jnp.float32),
             pltpu.SemaphoreType.DMA((2,)),
         ],
         compiler_params=pltpu.CompilerParams(vmem_limit_bytes=room << 20),

time: 466 us -> 465 us (level)
  no operation moved by 1% of the time
where the time goes in v3:
time: 465 us
  waiting for transfers between devices  163 us (35%)
  starting transfers between devices  159 us (34%)
  Pallas kernels  97.4 us (21%)
  local copies, waits for them, and re-layouts  39 us (8%)
    ppermute x27, waiting for transfers between devices, move(): return lax.ppermute(value, AXES, pairs)  155 us
    ppermute x27, starting transfers between devices, move(): return lax.ppermute(value, AXES, pairs)  131 us
    pallas_call x5, Pallas kernels, modes(): pl.pallas_call(functools.partial(mode_kernel, nev, tsrc, held, 64), out_s...  52.3 us
    pallas_call x4, Pallas kernels, inner_products(): pl.pallas_call(functools.partial(inner_kernel, nev, tsrc, slots, counts,...  42.9 us
    all_to_all x1, starting transfers between devices, chip_plan(): spread = lax.all_to_all(spread, AXES, 0, 0, tiled=True)  28.2 us
    dynamic_slice x3, local copies, waits for them, and re-layouts, send(): lax.dynamic_slice(after, (0, line, 0), (2, sizes[h], after.shape[2]))  12.9 us
    unnamed x42, local copies, waits for them, and re-layouts  11.4 us
  transfers between devices with their start and end apart: 28, of which 7 were waited for; matrix products, arithmetic and copies ran while one was open for 6% of the time, Pallas kernels for 18%

profile of v3, /device:TPU:0, one launch (start us, length us, event | category | flops | bytes accessed | tf_op | source)
XLA Modules:
  0.0 464.7 jit_solution(10128851015311794004)
XLA Ops:
  0.0 5.1 %collective-permute-start.2 = (bf16[2,2,64,512]{3,2,1,0:T(8,128)(2,1)}, bf16[2,2,64,512]{3,2,1,0:T(8,128)(2,1)S(1)}, u32[]{:S(2)}, u32[]{:S(2)}) collective-permute-start(bf16[2,2,64,512]{3,2,1,0:T(8,128)(2,1)} %bitcast.49), channel_id=1, source_target_pairs={{0,6},{1,7},{2,0},{3,1},{4,2},{5,3},{6,4},{7,5},{8,14},{9,15},{10,... | collective-permute-start | bytes 786440 | tf_op jit(solution)/shard_map/ppermute | solution.py:389
  8.8 4.3 constant_dynamic-slice_fusion
  17.9 33.4 %collective-permute-done.1 = bf16[2,2,64,512]{3,2,1,0:T(8,128)(2,1)S(1)} collective-permute-done((bf16[2,2,64,512]{3,2,1,0:T(8,128)(2,1)}, bf16[2,2,64,512]{3,2,1,0:T(8,128)(2,1)S(1)}, u32[]{:S(2)}, u32[]{:S(2)}) %collective-permute-start.1) | collective-permute-done | bytes 262176 | tf_op jit(solution)/shard_map/ppermute | solution.py:389
  55.7 40.6 %collective-permute-done.19.refs_24_.refs_32_ = bf16[2,2,128,1024]{3,2,1,0:T(8,128)(2,1)} collective-permute-done((bf16[2,2,128,1024]{3,2,1,0:T(8,128)(2,1)}, bf16[2,2,128,1024]{3,2,1,0:T(8,128)(2,1)}, u32[]{:S(2)}, u32[]{:S(2)}) %collective-permute-start.19) | collective-permute-done | bytes 1048608 | tf_op jit(solution)/shard_map/ppermute | solution.py:389
  99.4 41.8 %collective-permute-done.23.refs_36_ = bf16[2,2,128,1024]{3,2,1,0:T(8,128)(2,1)} collective-permute-done((bf16[2,2,128,1024]{3,2,1,0:T(8,128)(2,1)}, bf16[2,2,128,1024]{3,2,1,0:T(8,128)(2,1)}, u32[]{:S(2)}, u32[]{:S(2)}) %collective-permute-start.23) | collective-permute-done | bytes 1048608 | tf_op jit(solution)/shard_map/ppermute | solution.py:389
  144.4 4.7 %dynamic-slice_bitcast_fusion = (bf16[2,32,16384]{2,1,0:T(8,128)(2,1)}, bf16[2,32,16384]{2,1,0:T(8,128)(2,1)}) fusion(bf16[2,1,256,16384]{3,2,1,0:T(8,128)(2,1)} %param.5, s32[]{:T(128)S(6)} %select_n.193, s32[]{:T(128)S(6)} %select_n.192), kind=kLoop, calls=%fused_computation | loop fusion | bytes 8388616 | tf_op jit(solution)/shard_map/dynamic_slice | solution.py:406
  152.7 4.8 %constant_dynamic-slice_fusion.6 = (bf16[2,2,128,2048]{3,2,1,0:T(8,128)(2,1)}, bf16[2,2,128,2048]{3,2,1,0:T(8,128)(2,1)}) fusion(bf16[2,2,2048,2048]{3,2,1,0:T(8,128)(2,1)} %param.6, s32[]{:T(128)S(6)} %select_n.204, s32[]{:T(128)S(6)} %select_n.201), kind=kLoop, calls=%fused_computation.11 | loop fusion | bytes 8388616 | tf_op jit(solution)/shard_map/dynamic_slice | solution.py:415
  159.0 7.9 %collective-permute-start.16 = (bf16[2,2,128,2048]{3,2,1,0:T(8,128)(2,1)}, bf16[2,2,128,2048]{3,2,1,0:T(8,128)(2,1)}, u32[]{:S(2)}, u32[]{:S(2)}) collective-permute-start(bf16[2,2,128,2048]{3,2,1,0:T(8,128)(2,1)} %get-tuple-element.16.refs_8_.refs_4_.refs_20_.refs_28_), channel_id=1, source_target_pairs={{0,1},{1,0},{2,3},{3,2},{4,5},{5,4},{6,7},{7,6},{8,9},{9,8},{10,11... | collective-permute-start | bytes 6291464 | tf_op jit(solution)/shard_map/ppermute | solution.py:389
  168.5 22.9 %collective-permute-start.17 = (bf16[2,2,128,2048]{3,2,1,0:T(8,128)(2,1)}, bf16[2,2,128,2048]{3,2,1,0:T(8,128)(2,1)}, u32[]{:S(2)}, u32[]{:S(2)}) collective-permute-start(bf16[2,2,128,2048]{3,2,1,0:T(8,128)(2,1)} %get-tuple-element.15), channel_id=1, source_target_pairs={{0,2},{1,3},{2,4},{3,5},{4,6},{5,7},{6,0},{7,1},{8,10},{9,11},{10,... | collective-permute-start | bytes 6291464 | tf_op jit(solution)/shard_map/ppermute | solution.py:389
  197.0 24.8 %collective-permute-done.7.refs_3_ = bf16[768,256]{1,0:T(8,128)(2,1)S(1)} collective-permute-done((bf16[768,256]{1,0:T(8,128)(2,1)S(1)}, bf16[768,256]{1,0:T(8,128)(2,1)S(1)}, u32[]{:S(2)}, u32[]{:S(2)}) %collective-permute-start.7) | collective-permute-done | bytes 393248 | tf_op jit(solution)/shard_map/ppermute | solution.py:389
  226.3 13.2 %collective-permute-done.17.refs_10_.refs_6_.refs_22_.refs_30_ = bf16[2,2,128,2048]{3,2,1,0:T(8,128)(2,1)} collective-permute-done((bf16[2,2,128,2048]{3,2,1,0:T(8,128)(2,1)}, bf16[2,2,128,2048]{3,2,1,0:T(8,128)(2,1)}, u32[]{:S(2)}, u32[]{:S(2)}) %collective-permute-start.17) | collective-permute-done | bytes 2097184 | tf_op jit(solution)/shard_map/ppermute | solution.py:389
  242.3 30.1 %collective-permute-start.20 = (bf16[2,2,128,1024]{3,2,1,0:T(8,128)(2,1)}, bf16[2,2,128,1024]{3,2,1,0:T(8,128)(2,1)}, u32[]{:S(2)}, u32[]{:S(2)}) collective-permute-start(bf16[2,2,128,1024]{3,2,1,0:T(8,128)(2,1)} %collective-permute-done.19.refs_24_.refs_32_), channel_id=1, source_target_pairs={{0,1},{1,0},{2,3},{3,2},{4,5},{5,4},{6,7},{7,6},{8,9},{9,8},{10,11... | collective-permute-start | bytes 3145736 | tf_op jit(solution)/shard_map/ppermute | solution.py:389
  278.3 40.9 %collective-permute-start.24 = (bf16[2,2,128,1024]{3,2,1,0:T(8,128)(2,1)}, bf16[2,2,128,1024]{3,2,1,0:T(8,128)(2,1)}, u32[]{:S(2)}, u32[]{:S(2)}) collective-permute-start(bf16[2,2,128,1024]{3,2,1,0:T(8,128)(2,1)} %collective-permute-done.23.refs_36_), channel_id=1, source_target_pairs={{0,1},{1,0},{2,3},{3,2},{4,5},{5,4},{6,7},{7,6},{8,9},{9,8},{10,11... | collective-permute-start | bytes 3145736 | tf_op jit(solution)/shard_map/ppermute | solution.py:389
  328.0 8.0 %modes.5.refs_0_.refs_1_.refs_2_.refs_3_.refs_4_.refs_5_.refs_6_.refs_7_.refs_12_.refs_17_.refs_22_.refs_27_ = bf16[2,2,2,16,16384]{4,3,2,1,0:T(8,128)(2,1)} custom-call(s32[2]{0:T(128)} %get-tuple-element.31.info_ref, bf16[2,256,16384]{2,1,0:T(8,128)(2,1)} %bitcast.44, bf16[2,16,16384]{2,1,0:T(8,128)(2,1)} %collective-permute-done.3.refs_0_, ...), custom_call_target="tpu_custom_call" | custom-call | tf_op jit(solution)/shard_map/modes/pallas_call | solution.py:248
  336.0 7.9 %modes.9.refs_0_.refs_1_.refs_2_.refs_3_.refs_7_.refs_11_.refs_15_.refs_19_.refs_16_.refs_21_.refs_26_ = bf16[2,2,2,16,16384]{4,3,2,1,0:T(8,128)(2,1)} custom-call(s32[2]{0:T(128)} %pad_add_fusion.5.info_ref, bf16[2,256,16384]{2,1,0:T(8,128)(2,1)} %bitcast.45, bf16[2,16,16384]{2,1,0:T(8,128)(2,1)} %collective-permute-done.14.refs_0_, ...), custom_call_target="tpu_custom_call" | custom-call | tf_op jit(solution)/shard_map/modes/pallas_call | solution.py:248
  346.9 12.1 %modes.6.refs_0_.refs_2_.refs_4_.refs_6_.refs_8_.refs_12_.refs_16_.refs_13_.refs_18_.refs_23_ = bf16[2,2,2,32,16384]{4,3,2,1,0:T(8,128)(2,1)} custom-call(s32[2]{0:T(128)S(1)} %get-tuple-element.32.info_ref, bf16[2,256,16384]{2,1,0:T(8,128)(2,1)} %bitcast.46, bf16[2,32,16384]{2,1,0:T(8,128)(2,1)S(1)} %copy-done.4, ...), custom_call_target="tpu_custom_call" | custom-call | tf_op jit(solution)/shard_map/modes/pallas_call | solution.py:248
  359.1 12.3 %modes.7.refs_1_.refs_3_.refs_5_.refs_7_.refs_9_.refs_13_.refs_17_.refs_14_.refs_19_.refs_24_ = bf16[2,2,2,32,16384]{4,3,2,1,0:T(8,128)(2,1)} custom-call(s32[2]{0:T(128)S(1)} %get-tuple-element.33.info_ref, bf16[2,256,16384]{2,1,0:T(8,128)(2,1)} %bitcast.47, bf16[2,32,16384]{2,1,0:T(8,128)(2,1)S(1)} %copy-done.6, bf16[2,32,16384]{2,1,0:T(8,128)(2,1)S(1)} %copy-done.8, ...), custom_call_target="tpu_custom_call" | custom-call | tf_op jit(solution)/shard_map/modes/pallas_call | solution.py:248
  371.4 12.0 %modes.8.refs_0_.refs_1_.refs_2_.refs_3_.refs_6_.refs_10_.refs_14_.refs_18_.refs_15_.refs_20_.refs_25_ = bf16[2,2,2,32,16384]{4,3,2,1,0:T(8,128)(2,1)} custom-call(s32[2]{0:T(128)S(1)} %get-tuple-element.34.info_ref, bf16[2,256,16384]{2,1,0:T(8,128)(2,1)} %bitcast.48, bf16[2,32,16384]{2,1,0:T(8,128)(2,1)S(1)} %copy-done.10, ...), custom_call_target="tpu_custom_call" | custom-call | tf_op jit(solution)/shard_map/modes/pallas_call | solution.py:248
  384.0 8.9 %inner.4.refs_9_ = f32[8,128]{1,0:T(8,128)} custom-call(s32[4]{0:T(128)} %pad_add_fusion.6.where_ref, bf16[2,2,2,32,16384]{4,3,2,1,0:T(8,128)(2,1)} %modes.6.refs_0_.refs_2_.refs_4_.refs_6_.refs_8_.refs_12_.refs_16_.refs_13_.refs_18_.refs_23_, ...), custom_call_target="tpu_custom_call" | custom-call | tf_op jit(solution)/shard_map/inner/pallas_call | solution.py:351
  392.9 8.0 %inner.5.refs_29_ = f32[8,128]{1,0:T(8,128)} custom-call(s32[4]{0:T(128)} %pad_add_fusion.6.where_ref, bf16[2,2,2,32,16384]{4,3,2,1,0:T(8,128)(2,1)} %modes.8.refs_0_.refs_1_.refs_2_.refs_3_.refs_6_.refs_10_.refs_14_.refs_18_.refs_15_.refs_20_.refs_25_, ...), custom_call_target="tpu_custom_call" | custom-call | tf_op jit(solution)/shard_map/inner/pallas_call | solution.py:351
  400.9 11.8 %inner.6.refs_41_ = f32[8,128]{1,0:T(8,128)} custom-call(s32[8]{0:T(128)} %stack.158.where_ref, bf16[2,2,2,16,16384]{4,3,2,1,0:T(8,128)(2,1)} %modes.9.refs_0_.refs_1_.refs_2_.refs_3_.refs_7_.refs_11_.refs_15_.refs_19_.refs_16_.refs_21_.refs_26_, ...), custom_call_target="tpu_custom_call" | custom-call | tf_op jit(solution)/shard_map/inner/pallas_call | solution.py:351
  412.7 14.3 %inner.7 = f32[8,128]{1,0:T(8,128)} custom-call(s32[12]{0:T(128)} %stack.138.where_ref, bf16[2,2,2,16,16384]{4,3,2,1,0:T(8,128)(2,1)} %modes.5.refs_0_.refs_1_.refs_2_.refs_3_.refs_4_.refs_5_.refs_6_.refs_7_.refs_12_.refs_17_.refs_22_.refs_27_, ...), custom_call_target="tpu_custom_call" | custom-call | tf_op jit(solution)/shard_map/inner/pallas_call | solution.py:351
  428.2 28.2 %all-to-all-start = ((f32[32,1,128]{2,1,0:T(1,128)}), f32[32,1,128]{2,1,0:T(1,128)S(1)}, u32[]{:S(2)}, u32[]{:S(2)}) async-start(f32[32,1,128]{2,1,0:T(1,128)} %broadcast_in_dim.30), calls=%async_computation | async-start | bytes 32768 | tf_op jit(solution)/shard_map/all_to_all | solution.py:456
  456.5 7.1 %all-to-all-done = f32[32,1,128]{2,1,0:T(1,128)S(1)} async-done(((f32[32,1,128]{2,1,0:T(1,128)}), f32[32,1,128]{2,1,0:T(1,128)S(1)}, u32[]{:S(2)}, u32[]{:S(2)}) %all-to-all-start) | async-done | bytes 16416 | tf_op jit(solution)/shard_map/all_to_all | solution.py:456
  (112 shorter events, 56.9 us)
Async XLA Ops:
  5.1 46.2 %collective-permute-start.1 = (bf16[2,2,64,512]{3,2,1,0:T(8,128)(2,1)}, bf16[2,2,64,512]{3,2,1,0:T(8,128)(2,1)S(1)}, u32[]{:S(2)}, u32[]{:S(2)}) collective-permute-start(bf16[2,2,64,512]{3,2,1,0:T(8,128)(2,1)} %bitcast.50), channel_id=1, source_target_pairs={{0,4},{1,5},{2,6},{3,7},{4,0},{5,1},{6,2},{7,3},{8,12},{9,13},{10,... | collective-permute-start | bytes 786440 | tf_op jit(solution)/shard_map/ppermute | solution.py:389
  5.1 46.2 %collective-permute-start = (bf16[2,2,64,512]{3,2,1,0:T(8,128)(2,1)}, bf16[2,2,64,512]{3,2,1,0:T(8,128)(2,1)S(1)}, u32[]{:S(2)}, u32[]{:S(2)}) collective-permute-start(bf16[2,2,64,512]{3,2,1,0:T(8,128)(2,1)} %bitcast.51), channel_id=1, source_target_pairs={{0,2},{1,3},{2,4},{3,5},{4,6},{5,7},{6,0},{7,1},{8,10},{9,11},{10,... | collective-permute-start | bytes 786440 | tf_op jit(solution)/shard_map/ppermute | solution.py:389
  13.0 83.3 %collective-permute-start.19 = (bf16[2,2,128,1024]{3,2,1,0:T(8,128)(2,1)}, bf16[2,2,128,1024]{3,2,1,0:T(8,128)(2,1)}, u32[]{:S(2)}, u32[]{:S(2)}) collective-permute-start(bf16[2,2,128,1024]{3,2,1,0:T(8,128)(2,1)} %get-tuple-element.13), channel_id=1, source_target_pairs={{0,4},{1,5},{2,6},{3,7},{4,0},{5,1},{6,2},{7,3},{8,12},{9,13},{10,... | collective-permute-start | bytes 3145736 | tf_op jit(solution)/shard_map/ppermute | solution.py:389
  14.9 83.0 %collective-permute-start.21 = (bf16[2,2,128,1024]{3,2,1,0:T(8,128)(2,1)}, bf16[2,2,128,1024]{3,2,1,0:T(8,128)(2,1)}, u32[]{:S(2)}, u32[]{:S(2)}) collective-permute-start(bf16[2,2,128,1024]{3,2,1,0:T(8,128)(2,1)} %get-tuple-element.12), channel_id=1, source_target_pairs={{0,6},{1,7},{2,0},{3,1},{4,2},{5,3},{6,4},{7,5},{8,14},{9,15},{10,... | collective-permute-start | bytes 3145736 | tf_op jit(solution)/shard_map/ppermute | solution.py:389
  17.9 123.4 %collective-permute-start.23 = (bf16[2,2,128,1024]{3,2,1,0:T(8,128)(2,1)}, bf16[2,2,128,1024]{3,2,1,0:T(8,128)(2,1)}, u32[]{:S(2)}, u32[]{:S(2)}) collective-permute-start(bf16[2,2,128,1024]{3,2,1,0:T(8,128)(2,1)} %get-tuple-element.14), channel_id=1, source_target_pairs={{0,4},{1,5},{2,6},{3,7},{4,0},{5,1},{6,2},{7,3},{8,12},{9,13},{10,... | collective-permute-start | bytes 3145736 | tf_op jit(solution)/shard_map/ppermute | solution.py:389
  51.2 100.8 %collective-permute-start.25 = (bf16[2,2,128,1024]{3,2,1,0:T(8,128)(2,1)}, bf16[2,2,128,1024]{3,2,1,0:T(8,128)(2,1)}, u32[]{:S(2)}, u32[]{:S(2)}) collective-permute-start(bf16[2,2,128,1024]{3,2,1,0:T(8,128)(2,1)} %get-tuple-element.11), channel_id=1, source_target_pairs={{0,6},{1,7},{2,0},{3,1},{4,2},{5,3},{6,4},{7,5},{8,14},{9,15},{10,... | collective-permute-start | bytes 3145736 | tf_op jit(solution)/shard_map/ppermute | solution.py:389
  51.4 91.5 %collective-permute-start.5 = (bf16[4,2,2,64,512]{4,3,2,1,0:T(8,128)(2,1)S(1)}, bf16[4,2,2,64,512]{4,3,2,1,0:T(8,128)(2,1)S(1)}, u32[]{:S(2)}, u32[]{:S(2)}) collective-permute-start(bf16[4,2,2,64,512]{4,3,2,1,0:T(8,128)(2,1)S(1)} %pad_maximum_fusion.mine_ref), channel_id=1, source_target_pairs={{0,1},{1,0},{2,3},{3,2},{4,5},{5,4},{6,7},{7,6},{8,9},{9,8},{10,11... | collective-permute-start | bytes 3145736 | tf_op jit(solution)/shard_map/ppermute | solution.py:389
  96.3 61.2 %collective-permute-start.3 = (bf16[2,16,16384]{2,1,0:T(8,128)(2,1)}, bf16[2,16,16384]{2,1,0:T(8,128)(2,1)}, u32[]{:S(2)}, u32[]{:S(2)}) collective-permute-start(bf16[2,16,16384]{2,1,0:T(8,128)(2,1)} %get-tuple-element.20), channel_id=1, source_target_pairs={{1,16},{3,18},{5,20},{7,22},{9,24},{11,26},{13,28},{15,30},{16,1},... | collective-permute-start | bytes 3145736 | tf_op jit(solution)/shard_map/ppermute | solution.py:389
  98.0 60.4 %collective-permute-start.4 = (bf16[2,16,16384]{2,1,0:T(8,128)(2,1)}, bf16[2,16,16384]{2,1,0:T(8,128)(2,1)}, u32[]{:S(2)}, u32[]{:S(2)}) collective-permute-start(bf16[2,16,16384]{2,1,0:T(8,128)(2,1)} %get-tuple-element.19), channel_id=1, source_target_pairs={{0,8},{1,24},{2,10},{3,26},{4,12},{5,28},{6,14},{7,30},{8,0},{9,16... | collective-permute-start | bytes 3145736 | tf_op jit(solution)/shard_map/ppermute | solution.py:389
  152.0 39.4 %collective-permute-start.6 = (bf16[768,256]{1,0:T(8,128)(2,1)S(1)}, bf16[768,256]{1,0:T(8,128)(2,1)S(1)}, u32[]{:S(2)}, u32[]{:S(2)}) collective-permute-start(bf16[768,256]{1,0:T(8,128)(2,1)S(1)} %get-tuple-element.9.refs_0_), channel_id=1, source_target_pairs={{1,16},{3,18},{5,20},{7,22},{9,24},{11,26},{13,28},{15,30},{16,1},... | collective-permute-start | bytes 1179656 | tf_op jit(solution)/shard_map/ppermute | solution.py:389
  157.6 65.8 %collective-permute-start.8 = (bf16[2,32,16384]{2,1,0:T(8,128)(2,1)}, bf16[2,32,16384]{2,1,0:T(8,128)(2,1)S(1)}, u32[]{:S(2)}, u32[]{:S(2)}) collective-permute-start(bf16[2,32,16384]{2,1,0:T(8,128)(2,1)} %get-tuple-element.26), channel_id=1, source_target_pairs={{1,16},{3,18},{5,20},{7,22},{9,24},{11,26},{13,28},{15,30},{16,1},... | collective-permute-start | bytes 6291464 | tf_op jit(solution)/shard_map/ppermute | solution.py:389
  158.4 66.6 %collective-permute-start.9 = (bf16[2,32,16384]{2,1,0:T(8,128)(2,1)}, bf16[2,32,16384]{2,1,0:T(8,128)(2,1)}, u32[]{:S(2)}, u32[]{:S(2)}) collective-permute-start(bf16[2,32,16384]{2,1,0:T(8,128)(2,1)} %get-tuple-element.25), channel_id=1, source_target_pairs={{0,8},{1,24},{2,10},{3,26},{4,12},{5,28},{6,14},{7,30},{8,0},{9,16... | collective-permute-start | bytes 6291464 | tf_op jit(solution)/shard_map/ppermute | solution.py:389
  159.0 66.8 %collective-permute-start.16 = (bf16[2,2,128,2048]{3,2,1,0:T(8,128)(2,1)}, bf16[2,2,128,2048]{3,2,1,0:T(8,128)(2,1)}, u32[]{:S(2)}, u32[]{:S(2)}) collective-permute-start(bf16[2,2,128,2048]{3,2,1,0:T(8,128)(2,1)} %get-tuple-element.16.refs_8_.refs_4_.refs_20_.refs_28_), channel_id=1, source_target_pairs={{0,1},{1,0},{2,3},{3,2},{4,5},{5,4},{6,7},{7,6},{8,9},{9,8},{10,11... | collective-permute-start | bytes 6291464 | tf_op jit(solution)/shard_map/ppermute | solution.py:389
  168.5 70.9 %collective-permute-start.17 = (bf16[2,2,128,2048]{3,2,1,0:T(8,128)(2,1)}, bf16[2,2,128,2048]{3,2,1,0:T(8,128)(2,1)}, u32[]{:S(2)}, u32[]{:S(2)}) collective-permute-start(bf16[2,2,128,2048]{3,2,1,0:T(8,128)(2,1)} %get-tuple-element.15), channel_id=1, source_target_pairs={{0,2},{1,3},{2,4},{3,5},{4,6},{5,7},{6,0},{7,1},{8,10},{9,11},{10,... | collective-permute-start | bytes 6291464 | tf_op jit(solution)/shard_map/ppermute | solution.py:389
  191.4 30.3 %collective-permute-start.7 = (bf16[768,256]{1,0:T(8,128)(2,1)S(1)}, bf16[768,256]{1,0:T(8,128)(2,1)S(1)}, u32[]{:S(2)}, u32[]{:S(2)}) collective-permute-start(bf16[768,256]{1,0:T(8,128)(2,1)S(1)} %get-tuple-element.10.refs_1_), channel_id=1, source_target_pairs={{0,8},{1,24},{2,10},{3,26},{4,12},{5,28},{6,14},{7,30},{8,0},{9,16... | collective-permute-start | bytes 1179656 | tf_op jit(solution)/shard_map/ppermute | solution.py:389
  223.3 49.1 %collective-permute-start.11 = (bf16[2,32,16384]{2,1,0:T(8,128)(2,1)S(1)}, bf16[2,32,16384]{2,1,0:T(8,128)(2,1)S(1)}, u32[]{:S(2)}, u32[]{:S(2)}) collective-permute-start(bf16[2,32,16384]{2,1,0:T(8,128)(2,1)S(1)} %get-tuple-element.23), channel_id=1, source_target_pairs={{0,8},{1,24},{2,10},{3,26},{4,12},{5,28},{6,14},{7,30},{8,0},{9,16... | collective-permute-start | bytes 6291464 | tf_op jit(solution)/shard_map/ppermute | solution.py:389
  224.9 52.1 %collective-permute-start.12 = (bf16[2,32,16384]{2,1,0:T(8,128)(2,1)S(1)}, bf16[2,32,16384]{2,1,0:T(8,128)(2,1)S(1)}, u32[]{:S(2)}, u32[]{:S(2)}) collective-permute-start(bf16[2,32,16384]{2,1,0:T(8,128)(2,1)S(1)} %get-tuple-element.22), channel_id=1, source_target_pairs={{1,16},{3,18},{5,20},{7,22},{9,24},{11,26},{13,28},{15,30},{16,1},... | collective-permute-start | bytes 6291464 | tf_op jit(solution)/shard_map/ppermute | solution.py:389
  225.7 93.5 %collective-permute-start.13 = (bf16[2,32,16384]{2,1,0:T(8,128)(2,1)S(1)}, bf16[2,32,16384]{2,1,0:T(8,128)(2,1)S(1)}, u32[]{:S(2)}, u32[]{:S(2)}) collective-permute-start(bf16[2,32,16384]{2,1,0:T(8,128)(2,1)S(1)} %get-tuple-element.21), channel_id=1, source_target_pairs={{0,8},{1,24},{2,10},{3,26},{4,12},{5,28},{6,14},{7,30},{8,0},{9,16... | collective-permute-start | bytes 6291464 | tf_op jit(solution)/shard_map/ppermute | solution.py:389
  239.5 143.9 %collective-permute-start.18 = (bf16[2,2,128,2048]{3,2,1,0:T(8,128)(2,1)}, bf16[2,2,128,2048]{3,2,1,0:T(8,128)(2,1)}, u32[]{:S(2)}, u32[]{:S(2)}) collective-permute-start(bf16[2,2,128,2048]{3,2,1,0:T(8,128)(2,1)} %collective-permute-done.17.refs_10_.refs_6_.refs_22_.refs_30_), channel_id=1, source_target_pairs={{0,1},{1,0},{2,3},{3,2},{4,5},{5,4},{6,7},{7,6},{8,9},{9,8},{10,11... | collective-permute-start | bytes 6291464 | tf_op jit(solution)/shard_map/ppermute | solution.py:389
  242.3 158.5 %collective-permute-start.20 = (bf16[2,2,128,1024]{3,2,1,0:T(8,128)(2,1)}, bf16[2,2,128,1024]{3,2,1,0:T(8,128)(2,1)}, u32[]{:S(2)}, u32[]{:S(2)}) collective-permute-start(bf16[2,2,128,1024]{3,2,1,0:T(8,128)(2,1)} %collective-permute-done.19.refs_24_.refs_32_), channel_id=1, source_target_pairs={{0,1},{1,0},{2,3},{3,2},{4,5},{5,4},{6,7},{7,6},{8,9},{9,8},{10,11... | collective-permute-start | bytes 3145736 | tf_op jit(solution)/shard_map/ppermute | solution.py:389
  273.7 127.1 %collective-permute-start.22 = (bf16[2,2,128,1024]{3,2,1,0:T(8,128)(2,1)}, bf16[2,2,128,1024]{3,2,1,0:T(8,128)(2,1)}, u32[]{:S(2)}, u32[]{:S(2)}) collective-permute-start(bf16[2,2,128,1024]{3,2,1,0:T(8,128)(2,1)} %collective-permute-done.21.refs_26_.refs_34_), channel_id=1, source_target_pairs={{0,1},{1,0},{2,3},{3,2},{4,5},{5,4},{6,7},{7,6},{8,9},{9,8},{10,11... | collective-permute-start | bytes 3145736 | tf_op jit(solution)/shard_map/ppermute | solution.py:389
  278.3 134.3 %collective-permute-start.24 = (bf16[2,2,128,1024]{3,2,1,0:T(8,128)(2,1)}, bf16[2,2,128,1024]{3,2,1,0:T(8,128)(2,1)}, u32[]{:S(2)}, u32[]{:S(2)}) collective-permute-start(bf16[2,2,128,1024]{3,2,1,0:T(8,128)(2,1)} %collective-permute-done.23.refs_36_), channel_id=1, source_target_pairs={{0,1},{1,0},{2,3},{3,2},{4,5},{5,4},{6,7},{7,6},{8,9},{9,8},{10,11... | collective-permute-start | bytes 3145736 | tf_op jit(solution)/shard_map/ppermute | solution.py:389
  320.6 92.1 %collective-permute-start.26 = (bf16[2,2,128,1024]{3,2,1,0:T(8,128)(2,1)}, bf16[2,2,128,1024]{3,2,1,0:T(8,128)(2,1)}, u32[]{:S(2)}, u32[]{:S(2)}) collective-permute-start(bf16[2,2,128,1024]{3,2,1,0:T(8,128)(2,1)} %collective-permute-done.25.refs_38_), channel_id=1, source_target_pairs={{0,1},{1,0},{2,3},{3,2},{4,5},{5,4},{6,7},{7,6},{8,9},{9,8},{10,11... | collective-permute-start | bytes 3145736 | tf_op jit(solution)/shard_map/ppermute | solution.py:389
  428.2 35.4 %all-to-all-start = ((f32[32,1,128]{2,1,0:T(1,128)}), f32[32,1,128]{2,1,0:T(1,128)S(1)}, u32[]{:S(2)}, u32[]{:S(2)}) async-start(f32[32,1,128]{2,1,0:T(1,128)} %broadcast_in_dim.30), calls=%async_computation | async-start | bytes 32768 | tf_op jit(solution)/shard_map/all_to_all | solution.py:456
  (24 other events, 399.1 us)
